TPU v7x, 256 devices: a whole 4x4x8 slice. The times are simulated.
256 devices in a mesh: fsdp: 32 (over y, x, core), rep: 8 (over z).
Axes of the slice: x: 4, y: 4, z: 8, core: 2. Of those that a mesh axis runs over, the one named last changes fastest.
Arguments:
- tokens: bfloat16 [8, 4096, 2048], P('rep', 'fsdp'), may hold values from -6 to 6
- upstream: bfloat16 [8, 7168, 4096], P('rep', 'fsdp'), may hold values from -0.25 to 0.25
- weight: bfloat16 [2, 7168, 2048], P(None, 'fsdp'), may hold values from -0.125 to 0.125
- feedback: float32 [8, 2, 7168, 2048], P('rep', None, 'fsdp'), may hold values from -6 to 6
- momentum: float32 [2, 7168, 2048], P(None, 'fsdp', 'rep'), may hold values from -6 to 6
- right_factor: float32 [2, 7168, 64], P(None, 'fsdp'), may hold values from -6 to 6
Outputs:
- feedback_next: float32 [8, 2, 7168, 2048], P('rep', None, 'fsdp')
- momentum_next: float32 [2, 7168, 2048], P(None, 'fsdp', 'rep')
- weight_next: bfloat16 [2, 7168, 2048], P(None, 'fsdp', 'rep')
- right_next: float32 [2, 7168, 64], P(None, 'fsdp')
All inputs are finite; a program needn't handle non-finite values.
Results may differ from a plain program's by a relative error of at most 0.0023.
Values may be sent and summed in bfloat16 or wider, within the bound.
A program may use at most 128 MiB of HBM per device.

v0:
```python
import jax
import jax.numpy as jnp
from jax import lax
from jax.sharding import PartitionSpec as P

momentum_decay = 0.9
step_rate = 0.05
highest = lax.Precision.HIGHEST


def silu_pair(gate_pre):
    sigmoid = jax.nn.sigmoid(gate_pre)
    return (gate_pre * sigmoid, sigmoid * (1.0 + gate_pre * (1.0 - sigmoid)))


def solve_basis(factor, gram_matrix):
    lower_factor = jnp.linalg.cholesky(gram_matrix)
    return lax.linalg.triangular_solve(
        lower_factor, factor, left_side=False, lower=True, transpose_a=True
    )


def local_gram(factor):
    return jnp.einsum("kdr,kds->krs", factor, factor, precision=highest)


def per_device(tokens, upstream, weight, feedback, momentum, right_factor):
    own_rows = tokens[0]
    cotangents = upstream[0]
    contract_last = (((1,), (1,)), ((), ()))
    segment = lax.all_gather(own_rows, "fsdp", axis=0, tiled=True)
    cotangent_wide = cotangents.astype(jnp.float32)
    gate_pre = lax.dot_general(
        weight[0], segment, contract_last, preferred_element_type=jnp.float32
    )
    up_pre = lax.dot_general(weight[1], segment, contract_last, preferred_element_type=jnp.float32)
    activated, derivative = silu_pair(gate_pre)
    grad_gate = (cotangent_wide * up_pre * derivative).astype(jnp.bfloat16)
    grad_up = (cotangent_wide * activated).astype(jnp.bfloat16)
    term_gate = jnp.dot(grad_gate, segment, preferred_element_type=jnp.float32)
    term_up = jnp.dot(grad_up, segment, preferred_element_type=jnp.float32)
    gradient = jnp.stack([term_gate, term_up])
    delta = gradient + feedback[0]
    left_part = jnp.einsum("kfd,kfr->kdr", delta, right_factor, precision=highest)
    replicas = lax.axis_size("rep")
    left_mean = lax.psum(left_part, ("fsdp", "rep")) / replicas
    basis = solve_basis(left_mean, local_gram(left_mean))
    right_part = jnp.einsum("kfd,kdr->kfr", delta, basis, precision=highest)
    right_next = lax.psum(right_part, "rep") / replicas
    approx = jnp.einsum("kdr,kfr->kfd", basis, right_next, precision=highest)
    feedback_next = (delta - approx)[None]
    slab_cols = momentum.shape[2]
    slab_start = lax.axis_index("rep") * slab_cols
    approx_slab = lax.dynamic_slice_in_dim(approx, slab_start, slab_cols, 2)
    weight_slab = lax.dynamic_slice_in_dim(weight, slab_start, slab_cols, 2)
    momentum_next = momentum_decay * momentum + approx_slab
    weight_next = (weight_slab.astype(jnp.float32) - step_rate * momentum_next).astype(jnp.bfloat16)
    return (feedback_next, momentum_next, weight_next, right_next)


def solution(mesh):
    placed = (
        P("rep", "fsdp", None),
        P("rep", "fsdp", None),
        P(None, "fsdp", None),
        P("rep", None, "fsdp", None),
        P(None, "fsdp", "rep"),
        P(None, "fsdp", None),
    )
    return jax.shard_map(
        per_device,
        mesh=mesh,
        in_specs=placed,
        out_specs=(
            P("rep", None, "fsdp", None),
            P(None, "fsdp", "rep"),
            P(None, "fsdp", "rep"),
            P(None, "fsdp", None),
        ),
        check_vma=False,
    )
```

profile of v0, /device:TPU:1, one launch (start us, length us, event | category | flops | bytes accessed | tf_op | source)
XLA Modules:
  0.0 516.7 jit_solution(15495969798062645339)
XLA Ops:
  7.2 0.0 copy-start
  7.2 0.0 all-gather.3.cloned.1.call-start
  7.2 0.7 all-gather.3.cloned.1.call-update
  7.9 0.0 all-reduce.3.cloned.1.call-start
  8.0 84.4 %all-gather.3.cloned.1.call-done = bf16[1,4096,2048]{2,1,0:T(8,128)(2,1)} async-done(((bf16[1,128,2048]{2,1,0:T(8,128)(2,1)}), bf16[1,4096,2048]{2,1,0:T(8,128)(2,1)}) %all-gather.3.cloned.1.call-update) | async-done | bytes 16777232 | tf_op jit(solution)/shard_map/all_gather | solution.py:31
  92.3 13.1 %fusion.4 = f32[224,4096]{1,0:T(8,128)} fusion(bf16[1,4096,2048]{2,1,0:T(8,128)(2,1)} %all-gather.3.cloned.1.call-done, bf16[2,224,2048]{2,1,0:T(8,128)(2,1)} %param.8), kind=kOutput, calls=%fused_computation.4 | convolution fusion | flops 3758096384 | bytes 21364736 | tf_op jit(solution)/shard_map/dot_general | solution.py:33
  105.4 20.5 %fusion.25 = f32[1,224,2048]{2,1,0:T(8,128)S(1)} fusion(bf16[1,4096,2048]{2,1,0:T(8,128)(2,1)} %all-gather.3.cloned.1.call-done, f32[224,4096]{1,0:T(8,128)} %fusion.4, bf16[1,224,4096]{2,1,0:T(8,128)(2,1)} %param.7, bf16[2,224,2048]{2,1,0:T(8,128)(2,1)} %param.8), kind=kOutput, calls=%fused_computation.21 | convolution fusion | flops 7526285312 | bytes 41811968 | tf_op jit(solution)/shard_map/dot_general | solution.py:40
  125.9 0.0 copy-start.1
  125.9 9.7 %fusion.30 = f32[1,224,2048]{2,1,0:T(8,128)S(1)} fusion(bf16[1,4096,2048]{2,1,0:T(8,128)(2,1)} %all-gather.3.cloned.1.call-done, f32[224,4096]{1,0:T(8,128)} %fusion.4, bf16[1,224,4096]{2,1,0:T(8,128)(2,1)} %param.7), kind=kOutput, calls=%fused_computation.22 | convolution fusion | flops 3764518912 | bytes 24117248 | tf_op jit(solution)/shard_map/dot_general | solution.py:41
  135.7 0.0 copy-start.3
  135.7 1.2 copy-done.3
  136.9 0.0 copy-done
  137.0 0.0 copy-done.1
  137.0 3.6 fusion.57
  140.5 0.0 all-reduce.3.cloned.1.call-update
  140.6 0.2 all-reduce.5.cloned.1.call-start
  140.8 256.4 %all-reduce.3.cloned.1.call-done = f32[2,2048,64]{1,2,0:T(8,128)} async-done(((f32[2,2048,64]{1,2,0:T(8,128)}), f32[2,2048,64]{1,2,0:T(8,128)}) %all-reduce.3.cloned.1.call-update) | async-done | bytes 1048592 | tf_op jit(solution)/shard_map/psum | solution.py:46
  397.2 2.7 fusion.40
  399.9 0.1 copy.12
  400.0 11.7 %custom-call.7 = f32[2,64,64]{2,1,0:T(8,128)S(1)} custom-call(f32[2,64,64]{2,1,0:T(8,128)S(1)} %fusion.51), custom_call_target="Cholesky" | custom-call | tf_op jit(solution)/shard_map/jit(cholesky)/cholesky | solution.py:17
  411.8 0.1 compare_reduce_fusion
  411.9 0.1 select_bitcast_fusion
  412.0 9.8 %custom-call.8 = f32[2,1,64,64]{2,3,1,0:T(8,128)S(1)} custom-call(f32[2,1,64,64]{3,2,1,0:T(8,128)S(1)} %select_bitcast_fusion), custom_call_target="InvertDiagBlocksLowerTriangular" | custom-call | tf_op jit(solution)/shard_map/triangular_solve | solution.py:18
  421.8 2.3 fusion.38
  424.2 7.1 %fusion.56 = f32[2,224,64]{1,2,0:T(8,128)} fusion(f32[2,2048,64]{1,2,0:T(8,128)S(1)} %fusion.38, f32[1,224,2048]{2,1,0:T(8,128)} %copy-done.3, f32[1,224,2048]{2,1,0:T(8,128)S(1)} %fusion.25, f32[1,2,224,2048]{3,2,1,0:T(8,128)} %param.9), kind=kOutput, calls=%fused_computation.52 | convolution fusion | flops 706478080 | bytes 8503296 | tf_op jit(solution)/shard_map/kfd,kdr->kfr/dot_general | solution.py:48
  431.3 0.0 all-reduce.5.cloned.1.call-update
  431.3 68.0 %all-reduce.5.cloned.1.call-done = f32[2,224,64]{1,2,0:T(8,128)} async-done(((f32[2,224,64]{1,2,0:T(8,128)}), f32[2,224,64]{1,2,0:T(8,128)}) %all-reduce.5.cloned.1.call-update) | async-done | bytes 114704 | tf_op jit(solution)/shard_map/psum | solution.py:49
  499.2 0.0 copy-start.2
  499.3 1.1 broadcast_multiply_fusion
  500.3 0.0 copy-start.4
  500.3 3.1 fusion.58
  503.4 0.0 copy-done.2
  503.4 0.0 copy-start.5
  503.4 4.8 subtract_bitcast_fusion
  508.3 0.0 copy-done.4
  508.3 0.0 copy-done.5
  508.3 1.9 subtract_convert_fusion
  (4 shorter events, 0.1 us)
Async XLA Ops:
  7.2 129.8 %copy-start = (f32[2,224,64]{1,2,0:T(8,128)S(1)}, f32[2,224,64]{1,2,0:T(8,128)}, u32[]{:S(2)}) copy-start(f32[2,224,64]{1,2,0:T(8,128)} %param.11) | copy-start | bytes 344068
  7.2 85.1 %all-gather.3.cloned.1.call-start = ((), (), s32[]{:S(2)}) async-start(), calls=%async_computation.2 | async-start | bytes 17301504 | tf_op jit(solution)/shard_map/all_gather | solution.py:31
  7.9 389.3 %all-reduce.3.cloned.1.call-start = ((), (), s32[]{:S(2)}) async-start(), calls=%async_computation | async-start | bytes 2097152 | tf_op jit(solution)/shard_map/psum | solution.py:46
  125.9 11.0 %copy-start.1 = (f32[1,2,224,2048]{3,2,1,0:T(8,128)S(1)}, f32[1,2,224,2048]{3,2,1,0:T(8,128)}, u32[]{:S(2)}) copy-start(f32[1,2,224,2048]{3,2,1,0:T(8,128)} %param.9) | copy-start | bytes 11010052
  135.7 1.3 copy-start.3
  140.6 358.7 %all-reduce.5.cloned.1.call-start = ((), (), s32[]{:S(2)}) async-start(), calls=%async_computation.1 | async-start | bytes 262144 | tf_op jit(solution)/shard_map/psum | solution.py:49
  499.2 4.2 copy-start.2
  500.3 8.0 %copy-start.4 = (f32[2,224,64]{1,2,0:T(8,128)}, f32[2,224,64]{1,2,0:T(8,128)S(1)}, u32[]{:S(2)}) copy-start(f32[2,224,64]{1,2,0:T(8,128)S(1)} %broadcast_multiply_fusion) | copy-start | bytes 344068
  503.4 4.9 copy-start.5
Sparse Core Ops, SparseCore 0:
  10.5 81.7 all-gather.2
  140.7 256.5 all-reduce.2
  431.4 67.7 all-reduce.4
where the time goes:
time: 521 us; the launch traced here: 517 us
  waiting for transfers between devices  409 us (79%)
  matrix products  62.1 us (12%)
  other arithmetic  29.6 us (6%)
  between operations  13.9 us (3%)
    psum x1, waiting for transfers between devices, per_device(): left_mean = lax.psum(left_part, ('fsdp', 'rep')) / replicas  256 us
    all_gather x1, waiting for transfers between devices, per_device(): segment = lax.all_gather(own_rows, 'fsdp', axis=0, tiled=True)  84.4 us
    psum x1, waiting for transfers between devices, per_device(): right_next = lax.psum(right_part, 'rep') / replicas  68 us
    dot_general x1, matrix products, per_device(): term_gate = jnp.dot(grad_gate, segment, preferred_element_type=jnp.float32)  20.5 us
    dot_general x1, matrix products, per_device(): lax.dot_general(weight[0], segment, contract_last, preferred_element_type...  13.1 us
    another operation x4, other arithmetic, solve_basis(): lower_factor = jnp.linalg.cholesky(gram_matrix)  11.9 us
  transfers between devices with their start and end apart: 3, of which 3 were waited for; matrix products, arithmetic and copies ran while one was open for 0% of the time, Pallas kernels for 0%

commit v1 on v0

v1 whole, which is shorter than its diff:
```python
import functools

import jax
import jax.numpy as jnp
from jax import lax
from jax.experimental import pallas as pl
from jax.experimental.pallas import tpu as pltpu
from jax.sharding import PartitionSpec as P

momentum_decay = 0.9
step_rate = 0.05
highest = lax.Precision.HIGHEST
MESH = pl.DeviceIdType.MESH
F32 = jnp.float32
BF16 = jnp.bfloat16

CHUNK = 128
HALF = 64
DIM = 2048
HID = 224
RANK = 64
REPS = 8
SIDE = 4
NT = (((1,), (1,)), ((), ()))

ORDER = [
    (0, 0),
    (3, 0), (1, 0), (0, 3), (0, 1),
    (2, 0),
    (0, 2),
    (3, 3), (1, 1), (1, 3), (3, 1),
    (2, 3), (2, 1),
    (3, 2), (1, 2),
    (2, 2),
]
UNIT = {pos: i for i, pos in enumerate(ORDER)}
UNITS = len(ORDER)


def pick(table, u):
    out = jnp.int32(0)
    for i, v in enumerate(table):
        if v:
            out = out + jnp.where(u == i, jnp.int32(v), jnp.int32(0))
    return out


def step_kernel(
    tok_hbm, up_hbm, w_hbm, fb_hbm, rf_hbm,
    delta_out, left_out, aug_out, p_out,
    slots, acc, w, up, rf, r2t, dh, dl,
    snd_sib, rcv_sib, mine, recv1, s1, recv2, s2, recv3, full, psum, recv4, pfull, aug,
    in_sem, out_sem, ag_send, ag_recv, sib_send, sib_recv,
    a_send, a_recv, b_send, b_recv, c_send, c_recv, z_send, z_recv,
    gz_send, gz_recv, gb_send, gb_recv, gc_send, gc_recv, gs_send, gs_recv,
    pz_send, pz_recv, pg_send, pg_recv,
):
    f = lax.axis_index("fsdp")
    z = lax.axis_index("rep")
    c = lax.rem(f, 2)
    x = lax.rem(lax.div(f, 2), SIDE)
    y = lax.div(f, 2 * SIDE)
    p1 = x * (1 - c) + y * c
    p2 = y * (1 - c) + x * c
    t1 = 2 + 6 * c
    t2 = 8 - 6 * c

    def plane(q1, q2):
        return t1 * lax.rem(p1 + q1, SIDE) + t2 * lax.rem(p2 + q2, SIDE) + c

    def first_peer(off):
        return (plane(off, 0), z)

    def second_peer(off):
        return (plane(0, off), z)

    def rep_peer(off):
        return (f, lax.rem(z + off, REPS))

    sibling = (f + 1 - 2 * c, z)

    def remote(src, dst, ssem, rsem, dev):
        return pltpu.make_async_remote_copy(
            src_ref=src, dst_ref=dst, send_sem=ssem, recv_sem=rsem,
            device_id=dev, device_id_type=MESH,
        )

    load_tok = pltpu.make_async_copy(tok_hbm, slots.at[0, pl.ds(0, CHUNK), :], in_sem.at[0])
    load_tok.start()
    loads = [
        pltpu.make_async_copy(w_hbm, w, in_sem.at[1]),
        pltpu.make_async_copy(up_hbm, up, in_sem.at[2]),
        pltpu.make_async_copy(fb_hbm, acc, in_sem.at[3]),
        pltpu.make_async_copy(rf_hbm, rf, in_sem.at[4]),
    ]
    for copy in loads:
        copy.start()

    barrier = pltpu.get_barrier_semaphore()
    peers = [sibling]
    peers += [first_peer(o) for o in (1, 2, 3)]
    peers += [second_peer(o) for o in (1, 2, 3)]
    peers += [rep_peer(o) for o in range(1, REPS)]
    for dev in peers:
        pl.semaphore_signal(barrier, inc=1, device_id=dev, device_id_type=MESH)
    load_tok.wait()
    pl.semaphore_wait(barrier, len(peers))

    started = []

    def piece(d1, d2, h):
        return slots.at[UNIT[(d1, d2)], pl.ds(HALF * h, HALF), :]

    def send(d1, d2, h, axis, way):
        if axis == 1:
            r1, r2 = (d1 - way) % SIDE, d2
            dev = first_peer(way % SIDE)
        else:
            r1, r2 = d1, (d2 - way) % SIDE
            dev = second_peer(way % SIDE)
        copy = remote(
            piece(d1, d2, h), piece(r1, r2, h),
            ag_send.at[len(started)], ag_recv.at[UNIT[(r1, r2)], h], dev,
        )
        copy.start()
        started.append((d1, d2, h))

    def arrived(d1, d2, h):
        remote(
            piece(d1, d2, h), piece(d1, d2, h),
            ag_send.at[0], ag_recv.at[UNIT[(d1, d2)], h], sibling,
        ).wait_recv()

    def own_rows(u):
        return slots.at[u, pl.ds(0, CHUNK), :]

    def sib_rows(u):
        return slots.at[u, pl.ds(CHUNK, CHUNK), :]

    def share(d1, d2):
        u = UNIT[(d1, d2)]
        remote(own_rows(u), sib_rows(u), sib_send.at[u], sib_recv.at[u], sibling).start()

    send(0, 0, 0, 1, 1)
    send(0, 0, 1, 1, -1)
    share(0, 0)
    send(0, 0, 1, 1, 1)
    send(0, 0, 0, 1, -1)
    for copy in loads:
        copy.wait()

    for k in range(2):
        turned = jnp.transpose(rf[k], (1, 0))
        high = turned.astype(BF16)
        r2t[k, pl.ds(0, RANK), :] = high
        r2t[k, pl.ds(RANK, RANK), :] = (turned - high.astype(F32)).astype(BF16)

    def actions(u):
        if u == 0:
            arrived(3, 0, 0)
            arrived(1, 0, 1)
            send(3, 0, 0, 1, 1)
            send(1, 0, 1, 1, -1)
            send(0, 0, 0, 2, 1)
            send(0, 0, 1, 2, -1)
            send(0, 0, 1, 2, 1)
            send(0, 0, 0, 2, -1)
            send(3, 0, 0, 2, 1)
            send(1, 0, 1, 2, -1)
            send(1, 0, 1, 2, 1)
            send(3, 0, 0, 2, -1)
        if u == 1:
            arrived(3, 0, 1)
            arrived(1, 0, 0)
            share(3, 0)
            share(1, 0)
            arrived(0, 3, 0)
            arrived(0, 1, 1)
            send(0, 3, 0, 2, 1)
            send(0, 1, 1, 2, -1)
            send(3, 0, 1, 2, 1)
            send(1, 0, 0, 2, -1)
            send(1, 0, 0, 2, 1)
            send(3, 0, 1, 2, -1)
        if u == 3:
            arrived(0, 3, 1)
            arrived(0, 1, 0)
            share(0, 3)
            share(0, 1)
        if u == 4:
            arrived(2, 0, 0)
            arrived(2, 0, 1)
            share(2, 0)
            send(2, 0, 0, 2, 1)
            send(2, 0, 1, 2, -1)
        if u == 5:
            arrived(3, 3, 0)
            arrived(1, 1, 1)
            send(3, 3, 0, 2, 1)
            send(1, 1, 1, 2, -1)
            send(2, 0, 1, 2, 1)
            send(2, 0, 0, 2, -1)
        if u == 6:
            arrived(0, 2, 0)
            arrived(0, 2, 1)
            share(0, 2)
        if u == 7:
            arrived(3, 3, 1)
            arrived(1, 1, 0)
            share(3, 3)
            share(1, 1)
        if u == 9:
            arrived(1, 3, 0)
            arrived(3, 1, 1)
            send(1, 3, 0, 2, 1)
            send(3, 1, 1, 2, -1)
            arrived(1, 3, 1)
            arrived(3, 1, 0)
            share(1, 3)
            share(3, 1)
        if u == 10:
            arrived(2, 3, 0)
            arrived(2, 1, 1)
            send(2, 3, 0, 2, 1)
            send(2, 1, 1, 2, -1)
        if u == 11:
            arrived(2, 3, 1)
            arrived(2, 1, 0)
            share(2, 3)
            share(2, 1)
        if u == 13:
            arrived(3, 2, 0)
            arrived(1, 2, 1)
            arrived(3, 2, 1)
            arrived(1, 2, 0)
            share(3, 2)
            share(1, 2)
        if u == 15:
            arrived(2, 2, 0)
            arrived(2, 2, 1)
            share(2, 2)

    acting = (0, 1, 3, 4, 5, 6, 7, 9, 10, 11, 13, 15)
    first_of = [d1 for d1, _ in ORDER]
    second_of = [d2 for _, d2 in ORDER]

    def unit_step(u, carry):
        for i in acting:
            @pl.when(u == i)
            def _(i=i):
                actions(i)

        remote(own_rows(u), sib_rows(u), sib_send.at[u], sib_recv.at[u], sibling).wait_recv()
        d1, d2 = pick(first_of, u), pick(second_of, u)
        mine_f = plane(d1, d2)
        other_f = t2 * lax.rem(p2 + d1, SIDE) + t1 * lax.rem(p1 + d2, SIDE) + (1 - c)
        cot_mine = up[:, pl.ds(pl.multiple_of(mine_f * CHUNK, CHUNK), CHUNK)]
        cot_other = up[:, pl.ds(pl.multiple_of(other_f * CHUNK, CHUNK), CHUNK)]
        cot = jnp.concatenate([cot_mine, cot_other], axis=1).astype(F32)
        rows = slots[u]
        pre = lax.dot_general(w[...], rows, NT, preferred_element_type=F32)
        gate_pre, up_pre = pre[:HID], pre[HID:]
        sig = jax.nn.sigmoid(gate_pre)
        grad_gate = (cot * up_pre * (sig * (1.0 + gate_pre * (1.0 - sig)))).astype(BF16)
        grad_up = (cot * (gate_pre * sig)).astype(BF16)
        grads = jnp.concatenate([grad_gate, grad_up], axis=0)
        acc[...] += jnp.dot(grads, rows, preferred_element_type=F32)
        return carry

    lax.fori_loop(0, UNITS, unit_step, 0)

    assert len(started) == AG_SENDS
    stores = [pltpu.make_async_copy(acc, delta_out, out_sem.at[0])]
    stores[0].start()

    def left_part(k, g, dst):
        cols = pl.ds(pl.multiple_of(512 * g, 512) if not isinstance(g, int) else 512 * g, 512)
        kr = pl.ds(pl.multiple_of(HID * k, 32), HID)
        block = acc[kr, cols]
        high = block.astype(BF16)
        low = (block - high.astype(F32)).astype(BF16)
        dh[kr, cols] = high
        dl[kr, cols] = low
        both = jnp.dot(r2t[k], high, preferred_element_type=F32)
        part = both[:RANK] + both[RANK:]
        part = part + jnp.dot(r2t[k, pl.ds(0, RANK), :], low, preferred_element_type=F32)
        for i in range(4):
            dst[4 * g + i] = part[:, 128 * i : 128 * (i + 1)]

    for g in range(4):
        left_part(1 - c, g, snd_sib)
        remote(
            snd_sib.at[pl.ds(4 * g, 4)], rcv_sib.at[pl.ds(4 * g, 4)],
            a_send.at[g], a_recv.at[g], sibling,
        ).start()
    for g in range(4):
        left_part(c, g, mine)
    for g in range(4):
        remote(
            snd_sib.at[pl.ds(4 * g, 4)], rcv_sib.at[pl.ds(4 * g, 4)],
            a_send.at[g], a_recv.at[g], sibling,
        ).wait()

    def first_copy(off):
        q = lax.rem(p1 + off, SIDE)
        return remote(
            mine.at[pl.ds(4 * q, 4)], recv1.at[off - 1],
            b_send.at[off - 1], b_recv.at[off - 1], first_peer(off),
        )

    for off in (2, 1, 3):
        q = lax.rem(p1 + off, SIDE)
        mine[pl.ds(4 * q, 4)] += rcv_sib[pl.ds(4 * q, 4)]
        first_copy(off).start()
    total = mine[pl.ds(4 * p1, 4)] + rcv_sib[pl.ds(4 * p1, 4)]
    for off in (1, 3, 2):
        first_copy(off).wait_recv()
        total = total + recv1[off - 1]
    s1[...] = total

    def second_copy(off):
        q = lax.rem(p2 + off, SIDE)
        return remote(
            s1.at[q], recv2.at[off - 1],
            c_send.at[off - 1], c_recv.at[off - 1], second_peer(off),
        )

    for off in (2, 1, 3):
        second_copy(off).start()
    total = s1[p2]
    for off in (1, 3, 2):
        second_copy(off).wait_recv()
        total = total + recv2[off - 1]
    s2[...] = total

    far_first = (4, 3, 5, 2, 6, 1, 7)

    def rep_copy(off):
        q = lax.rem(z + off, REPS)
        return remote(
            s2.at[pl.ds(pl.multiple_of(8 * q, 8), 8), :], recv3.at[off - 1],
            z_send.at[off - 1], z_recv.at[off - 1], rep_peer(off),
        )

    for off in far_first:
        rep_copy(off).start()
    total = s2[pl.ds(pl.multiple_of(8 * z, 8), 8), :]
    for off in reversed(far_first):
        rep_copy(off).wait_recv()
        total = total + recv3[off - 1]

    b = 4 * p1 + p2
    own_piece = full.at[c, b, pl.ds(pl.multiple_of(8 * z, 8), 8), :]
    own_piece[...] = total * (1.0 / REPS)

    def rep_gather(off):
        return remote(own_piece, own_piece, gz_send.at[off - 1], gz_recv.at[off - 1], rep_peer(off))

    for off in far_first:
        rep_gather(off).start()
    for off in reversed(far_first):
        rep_gather(off).wait_recv()

    def second_gather(off):
        return remote(
            full.at[c, b], full.at[c, b],
            gb_send.at[off - 1], gb_recv.at[off - 1], second_peer(off),
        )

    for off in (2, 1, 3):
        second_gather(off).start()
    for off in (1, 3, 2):
        second_gather(off).wait_recv()

    def first_gather(off):
        group = full.at[c, pl.ds(4 * p1, 4)]
        return remote(group, group, gc_send.at[off - 1], gc_recv.at[off - 1], first_peer(off))

    def pass_on(off):
        q = lax.rem(p1 + 4 - off, SIDE)
        group = full.at[c, pl.ds(4 * q, 4)]
        return remote(group, group, gs_send.at[off], gs_recv.at[off], sibling)

    for off in (2, 1, 3):
        first_gather(off).start()
    pass_on(0).start()
    for off in (1, 3, 2):
        first_gather(off).wait_recv()
        pass_on(off).start()

    lane = lax.broadcasted_iota(jnp.int32, (RANK, 128), 1)
    row = lax.broadcasted_iota(jnp.int32, (RANK, 128), 0)

    def left_rows(k):
        return jnp.concatenate([full[k, i] for i in range(16)], axis=1)

    def product(k):
        left = left_rows(k)
        high = left.astype(BF16)
        low = (left - high.astype(F32)).astype(BF16)
        kr = pl.ds(pl.multiple_of(HID * k, 32), HID)
        part = lax.dot_general(
            dh[kr, :], jnp.concatenate([high, low], axis=0), NT, preferred_element_type=F32
        )
        part = part + pltpu.roll(part, RANK, 1)
        return part + lax.dot_general(
            dl[kr, :], jnp.concatenate([high, high], axis=0), NT, preferred_element_type=F32
        )

    prod_own = product(c)
    for off in range(4):
        pass_on(off).wait()
    prod_other = product(1 - c)
    wide = lax.broadcasted_iota(jnp.int32, (HID, 128), 1)
    low_lanes = (wide < RANK) == (c == 0)
    psum[pl.ds(0, HID), :] = jnp.where(low_lanes, prod_own, prod_other)
    psum[pl.ds(HID, 32), :] = jnp.zeros((32, 128), F32)

    def p_rows(i):
        return pl.ds(pl.multiple_of(32 * i, 32), 32)

    def p_copy(off):
        q = lax.rem(z + off, REPS)
        return remote(
            psum.at[p_rows(q), :], recv4.at[off - 1],
            pz_send.at[off - 1], pz_recv.at[off - 1], rep_peer(off),
        )

    for off in far_first:
        p_copy(off).start()
    store_left = pltpu.make_async_copy(full, left_out, out_sem.at[1])
    store_left.start()

    for k in range(2):
        left = left_rows(k)
        padded = jnp.concatenate([left, jnp.zeros_like(left)], axis=0)
        gram = lax.dot_general(left, padded, NT, precision=highest, preferred_element_type=F32)
        aug[k] = jnp.where(lane == row + RANK, 1.0, gram)

    def eliminate(j, carry):
        for k in range(2):
            table = aug[k]
            pivot_row = aug[k, pl.ds(j, 1), :]
            at_j = lane == j
            pivot = jnp.sum(jnp.where(at_j[:1], pivot_row, 0.0), axis=1, keepdims=True)
            column = jnp.sum(jnp.where(at_j, table, 0.0), axis=1, keepdims=True)
            inv = lax.rsqrt(pivot)
            scaled = pivot_row * inv
            factor = column * inv
            aug[k] = jnp.where(
                row > j, table - factor * scaled, jnp.where(row == j, scaled, table)
            )
        return carry

    lax.fori_loop(0, RANK // 2, eliminate, 0)

    total = psum[p_rows(z), :]
    for off in reversed(far_first):
        p_copy(off).wait_recv()
        total = total + recv4[off - 1]
    pfull[p_rows(z), :] = total * (1.0 / REPS)

    def p_gather(off):
        group = pfull.at[p_rows(z), :]
        return remote(group, group, pg_send.at[off - 1], pg_recv.at[off - 1], rep_peer(off))

    for off in far_first:
        p_gather(off).start()

    lax.fori_loop(RANK // 2, RANK, eliminate, 0)
    aug_out[...] = aug[...]

    for off in reversed(far_first):
        p_gather(off).wait_recv()
    p_out[...] = pfull[...]

    for i, (d1, d2, h) in enumerate(started):
        remote(
            piece(d1, d2, h), piece(d1, d2, h), ag_send.at[i], ag_recv.at[0, 0], sibling
        ).wait_send()
    for u in range(UNITS):
        remote(own_rows(u), sib_rows(u), sib_send.at[u], sib_recv.at[u], sibling).wait_send()
    for off in (1, 2, 3):
        first_copy(off).wait_send()
        second_copy(off).wait_send()
        second_gather(off).wait_send()
        first_gather(off).wait_send()
    for off in far_first:
        rep_copy(off).wait_send()
        rep_gather(off).wait_send()
        p_copy(off).wait_send()
        p_gather(off).wait_send()
    stores[0].wait()
    store_left.wait()


AG_SENDS = 30


def step_call(tokens, upstream, weight, feedback, right_factor):
    any_space = pl.BlockSpec(memory_space=pl.ANY)
    vmem = pl.BlockSpec(memory_space=pltpu.VMEM)
    dma = pltpu.SemaphoreType.DMA
    return pl.pallas_call(
        step_kernel,
        name="gather_reduce",
        out_shape=(
            jax.ShapeDtypeStruct((2 * HID, DIM), F32),
            jax.ShapeDtypeStruct((2, 16, RANK, 128), F32),
            jax.ShapeDtypeStruct((2, RANK, 128), F32),
            jax.ShapeDtypeStruct((256, 128), F32),
        ),
        in_specs=[any_space] * 5,
        out_specs=(any_space, any_space, vmem, vmem),
        scratch_shapes=[
            pltpu.VMEM((UNITS, 2 * CHUNK, DIM), BF16),
            pltpu.VMEM((2 * HID, DIM), F32),
            pltpu.VMEM((2 * HID, DIM), BF16),
            pltpu.VMEM((HID, 32 * CHUNK), BF16),
            pltpu.VMEM((2, HID, RANK), F32),
            pltpu.VMEM((2, 2 * RANK, HID), BF16),
            pltpu.VMEM((2 * HID, DIM), BF16),
            pltpu.VMEM((2 * HID, DIM), BF16),
            pltpu.VMEM((16, RANK, 128), F32),
            pltpu.VMEM((16, RANK, 128), F32),
            pltpu.VMEM((16, RANK, 128), F32),
            pltpu.VMEM((3, 4, RANK, 128), F32),
            pltpu.VMEM((4, RANK, 128), F32),
            pltpu.VMEM((3, RANK, 128), F32),
            pltpu.VMEM((RANK, 128), F32),
            pltpu.VMEM((7, 8, 128), F32),
            pltpu.VMEM((2, 16, RANK, 128), F32),
            pltpu.VMEM((256, 128), F32),
            pltpu.VMEM((7, 32, 128), F32),
            pltpu.VMEM((256, 128), F32),
            pltpu.VMEM((2, RANK, 128), F32),
            dma((5,)), dma((2,)),
            dma((AG_SENDS,)), dma((UNITS, 2)), dma((UNITS,)), dma((UNITS,)),
            dma((4,)), dma((4,)), dma((3,)), dma((3,)), dma((3,)), dma((3,)), dma((7,)), dma((7,)),
            dma((7,)), dma((7,)), dma((3,)), dma((3,)), dma((3,)), dma((3,)), dma((4,)), dma((4,)),
            dma((7,)), dma((7,)), dma((7,)), dma((7,)),
        ],
        compiler_params=pltpu.CompilerParams(
            collective_id=0, has_side_effects=True, vmem_limit_bytes=60 * 1024 * 1024
        ),
    )(
        tokens.reshape(CHUNK, DIM),
        upstream.reshape(HID, 32 * CHUNK),
        weight.reshape(2 * HID, DIM),
        feedback.reshape(2 * HID, DIM),
        right_factor,
    )


COLS = 256


def finish_kernel(
    z_ref, delta, left, aug, p, momentum, weight, fb_out, mom_out, w_out, right_out, coef
):
    j = pl.program_id(0)

    @pl.when(j == 0)
    def _():
        lane = lax.broadcasted_iota(jnp.int32, (RANK, 128), 1)
        for k in range(2):
            turned = jnp.where(lane < RANK, pltpu.roll(aug[k], RANK, 1), 0.0)
            placed = turned if k == 0 else jnp.where(lane >= RANK, aug[k], 0.0)
            right = lax.dot_general(
                p[pl.ds(0, HID), :], placed, NT, precision=highest, preferred_element_type=F32
            )
            right_out[k] = right
            coef[k] = jnp.dot(right, turned, precision=highest, preferred_element_type=F32)[:, :RANK]

    for k in range(2):
        block = jnp.concatenate([left[k, 0], left[k, 1]], axis=1)
        approx = jnp.dot(coef[k], block, precision=highest, preferred_element_type=F32)
        fb_out[k] = delta[k] - approx

        @pl.when(j == z_ref[0])
        def _(k=k, approx=approx):
            moved = momentum_decay * momentum[k] + approx
            mom_out[k] = moved
            w_out[k] = (weight[k].astype(F32) - step_rate * moved).astype(BF16)


def finish_call(slab, delta, left, aug, p, momentum, weight):
    whole = lambda *shape: pl.BlockSpec(shape, lambda j, s: (0,) * len(shape))
    return pl.pallas_call(
        finish_kernel,
        name="finish",
        grid_spec=pltpu.PrefetchScalarGridSpec(
            num_scalar_prefetch=1,
            grid=(DIM // COLS,),
            in_specs=[
                pl.BlockSpec((2, HID, COLS), lambda j, s: (0, 0, j)),
                pl.BlockSpec((2, 2, RANK, 128), lambda j, s: (0, j, 0, 0)),
                whole(2, RANK, 128),
                whole(256, 128),
                whole(2, HID, COLS),
                pl.BlockSpec((2, HID, COLS), lambda j, s: (0, 0, s[0])),
            ],
            out_specs=[
                pl.BlockSpec((2, HID, COLS), lambda j, s: (0, 0, j)),
                whole(2, HID, COLS),
                whole(2, HID, COLS),
                whole(2, HID, RANK),
            ],
            scratch_shapes=[pltpu.VMEM((2, HID, RANK), F32)],
        ),
        out_shape=(
            jax.ShapeDtypeStruct((2, HID, DIM), F32),
            jax.ShapeDtypeStruct((2, HID, COLS), F32),
            jax.ShapeDtypeStruct((2, HID, COLS), BF16),
            jax.ShapeDtypeStruct((2, HID, RANK), F32),
        ),
        compiler_params=pltpu.CompilerParams(dimension_semantics=("arbitrary",)),
    )(slab, delta, left, aug, p, momentum, weight)


def per_device(tokens, upstream, weight, feedback, momentum, right_factor):
    delta, left, aug, p = step_call(tokens, upstream, weight, feedback, right_factor)
    slab = lax.axis_index("rep").astype(jnp.int32).reshape(1)
    feedback_next, momentum_next, weight_next, right_next = finish_call(
        slab, delta.reshape(2, HID, DIM), left, aug, p, momentum, weight
    )
    return (feedback_next[None], momentum_next, weight_next, right_next)


def solution(mesh):
    placed = (
        P("rep", "fsdp", None),
        P("rep", "fsdp", None),
        P(None, "fsdp", None),
        P("rep", None, "fsdp", None),
        P(None, "fsdp", "rep"),
        P(None, "fsdp", None),
    )
    return jax.shard_map(
        per_device,
        mesh=mesh,
        in_specs=placed,
        out_specs=(
            P("rep", None, "fsdp", None),
            P(None, "fsdp", "rep"),
            P(None, "fsdp", "rep"),
            P(None, "fsdp", None),
        ),
        check_vma=False,
    )
```

time: 521 us -> 137 us (0.26)
  waiting for transfers between devices: 409 us -> 0 us
  Pallas kernels: 0 us -> 133 us
  matrix products: 62.1 us -> 0 us
  other arithmetic: 29.6 us -> 0 us
  between operations: 13.9 us -> 0.64 us
    psum x2 -> x0, waiting for transfers between devices: 324 us -> none  [the longest x1 256 us: per_device(): left_mean = lax.psum(left_part, ('fsdp', 'rep')) / replicas]
    pallas_call x0 -> x2, Pallas kernels: none -> 133 us  [the longest x1 121 us: step_call(): pl.pallas_call(step_kernel, name='gather_reduce', out_shape=(jax.ShapeDty...]
    all_gather x1 -> x0, waiting for transfers between devices: 84.4 us -> none  [per_device(): segment = lax.all_gather(own_rows, 'fsdp', axis=0, tiled=True)]
    dot_general x7 -> x0, matrix products: 59.8 us -> none  [the longest x1 20.5 us: per_device(): term_gate = jnp.dot(grad_gate, segment, preferred_element_type=jnp.float32)]
    another operation x7 -> x0, other arithmetic: 21.8 us -> none  [the longest x4 11.9 us: solve_basis(): lower_factor = jnp.linalg.cholesky(gram_matrix)]
  transfers between devices with their start and end apart: 3 -> 0, of which waited for: 3 -> 0; matrix products, arithmetic and copies ran while one was open for 0% -> 0% of each run, Pallas kernels for 0% -> 0%
where the time goes in v1:
time: 137 us
  Pallas kernels  133 us (97%)
  local copies, waits for them, and re-layouts  3.44 us (3%)
    pallas_call x1, Pallas kernels, step_call(): pl.pallas_call(step_kernel, name='gather_reduce', out_shape=(jax.ShapeDty...  121 us
    pallas_call x1, Pallas kernels, finish_call(): pl.pallas_call(finish_kernel, name='finish', grid_spec=pltpu.PrefetchScal...  12.3 us
    unnamed x2, local copies, waits for them, and re-layouts  3.44 us

profile of v1, /device:TPU:1, one launch (start us, length us, event | category | flops | bytes accessed | tf_op | source)
XLA Modules:
  0.0 136.9 jit_solution(17134461409219589539)
XLA Ops:
  0.6 1.7 %copy.10.rf_hbm = f32[2,224,64]{2,1,0:T(8,128)} copy(f32[2,224,64]{1,2,0:T(8,128)} %param.11) | data formatting | bytes 229376 | tf_op args[5]
  2.4 120.6 %gather_reduce.1 = (f32[448,2048]{1,0:T(8,128)}, f32[2,16,64,128]{3,2,1,0:T(8,128)}, f32[2,64,128]{2,1,0:T(8,128)}, f32[256,128]{1,0:T(8,128)}) custom-call(bf16[128,2048]{1,0:T(8,128)(2,1)} %bitcast.11, bf16[224,4096]{1,0:T(8,128)(2,1)} %bitcast.10, bf16[448,2048]{1,0:T(8,128)(2,1)} %bitcast.7, f32[448,2048]{1,0:T(8,128)} %bitcast.9, f32[2,224,64]{2,1,0:T(8,128)} %copy.10.rf_hbm), custom_call_target="tpu_custom_call" | custom-call | tf_op jit(solution)/shard_map/gather_reduce/pallas_call | solution.py:504
  122.9 12.3 %finish.1 = (f32[2,224,2048]{2,1,0:T(8,128)}, f32[2,224,256]{2,1,0:T(8,128)}, bf16[2,224,256]{2,1,0:T(8,128)(2,1)}, f32[2,224,64]{2,1,0:T(8,128)}) custom-call(s32[1]{0:T(128)} %bitcast.z_ref, f32[2,224,2048]{2,1,0:T(8,128)} %bitcast.8, f32[2,16,64,128]{3,2,1,0:T(8,128)} %get-tuple-element.13.left, f32[2,64,128]{2,1,0:T(8,128)} %get-tuple-element.14.aug, ...), custom_call_target="tpu_custom_call" | custom-call | tf_op jit(solution)/shard_map/finish/pallas_call | solution.py:589
  135.2 1.7 %copy.11 = f32[2,224,64]{1,2,0:T(8,128)} copy(f32[2,224,64]{2,1,0:T(8,128)} %get-tuple-element.23) | data formatting | bytes 229376

commit v2 on v1

v2 whole, which is shorter than its diff:
```python
import functools

import jax
import jax.numpy as jnp
from jax import lax
from jax.experimental import pallas as pl
from jax.experimental.pallas import tpu as pltpu
from jax.sharding import PartitionSpec as P

momentum_decay = 0.9
step_rate = 0.05
highest = lax.Precision.HIGHEST
MESH = pl.DeviceIdType.MESH
F32 = jnp.float32
BF16 = jnp.bfloat16

CHUNK = 128
HALF = 64
DIM = 2048
HID = 224
RANK = 64
REPS = 8
SIDE = 4
NT = (((1,), (1,)), ((), ()))

ORDER = [
    (0, 0), (3, 0),
    (1, 0), (0, 3),
    (0, 1), (2, 0),
    (0, 2), (3, 3),
    (1, 1), (1, 3),
    (3, 1), (2, 3),
    (2, 1), (3, 2),
    (1, 2), (2, 2),
]
UNIT = {pos: i for i, pos in enumerate(ORDER)}
UNITS = len(ORDER)
PAIRS = UNITS // 2


def pick(table, u):
    out = jnp.int32(0)
    for i, v in enumerate(table):
        if v:
            out = out + jnp.where(u == i, jnp.int32(v), jnp.int32(0))
    return out


def step_kernel(
    tok_hbm, up_hbm, w_hbm, fb_hbm, rf_hbm,
    delta_out, left_out, solve_out, p_out,
    slots, acc, w, up, rf, r2t, dsplit,
    snd_sib, rcv_sib, mine, recv1, s1, recv2, s2, recv3, whole, full, psum, recv4, pfull, aug,
    in_sem, out_sem, ag_send, ag_recv, sib_send, sib_recv,
    a_send, a_recv, b_send, b_recv, c_send, c_recv, z_send, z_recv,
    gz_send, gz_recv, gb_send, gb_recv, gc_send, gc_recv, gs_send, gs_recv,
    pz_send, pz_recv, pg_send, pg_recv,
):
    f = lax.axis_index("fsdp")
    z = lax.axis_index("rep")
    c = lax.rem(f, 2)
    x = lax.rem(lax.div(f, 2), SIDE)
    y = lax.div(f, 2 * SIDE)
    p1 = x * (1 - c) + y * c
    p2 = y * (1 - c) + x * c
    t1 = 2 + 6 * c
    t2 = 8 - 6 * c

    def plane(q1, q2):
        return t1 * lax.rem(p1 + q1, SIDE) + t2 * lax.rem(p2 + q2, SIDE) + c

    def first_peer(off):
        return (plane(off, 0), z)

    def second_peer(off):
        return (plane(0, off), z)

    def rep_peer(off):
        return (f, lax.rem(z + off, REPS))

    sibling = (f + 1 - 2 * c, z)

    def remote(src, dst, ssem, rsem, dev):
        return pltpu.make_async_remote_copy(
            src_ref=src, dst_ref=dst, send_sem=ssem, recv_sem=rsem,
            device_id=dev, device_id_type=MESH,
        )

    load_tok = pltpu.make_async_copy(tok_hbm, slots.at[0, pl.ds(0, CHUNK), :], in_sem.at[0])
    load_tok.start()
    loads = [
        pltpu.make_async_copy(w_hbm, w, in_sem.at[1]),
        pltpu.make_async_copy(up_hbm, up, in_sem.at[2]),
        pltpu.make_async_copy(fb_hbm, acc, in_sem.at[3]),
        pltpu.make_async_copy(rf_hbm, rf, in_sem.at[4]),
    ]
    for copy in loads:
        copy.start()

    barrier = pltpu.get_barrier_semaphore()
    peers = [sibling]
    peers += [first_peer(o) for o in (1, 2, 3)]
    peers += [second_peer(o) for o in (1, 2, 3)]
    peers += [rep_peer(o) for o in range(1, REPS)]
    for dev in peers:
        pl.semaphore_signal(barrier, inc=1, device_id=dev, device_id_type=MESH)
    load_tok.wait()
    pl.semaphore_wait(barrier, len(peers))

    started = []

    def piece(d1, d2, h):
        u = UNIT[(d1, d2)]
        return slots.at[u // 2, pl.ds(2 * CHUNK * (u % 2) + HALF * h, HALF), :]

    def send(d1, d2, h, axis, way):
        if axis == 1:
            r1, r2 = (d1 - way) % SIDE, d2
            dev = first_peer(way % SIDE)
        else:
            r1, r2 = d1, (d2 - way) % SIDE
            dev = second_peer(way % SIDE)
        copy = remote(
            piece(d1, d2, h), piece(r1, r2, h),
            ag_send.at[len(started)], ag_recv.at[UNIT[(r1, r2)], h], dev,
        )
        copy.start()
        started.append((d1, d2, h))

    def arrived(d1, d2, h):
        remote(
            piece(d1, d2, h), piece(d1, d2, h),
            ag_send.at[0], ag_recv.at[UNIT[(d1, d2)], h], sibling,
        ).wait_recv()

    def sib_copy(u, half):
        start = 2 * CHUNK * half
        pair = slots.at[lax.div(u, 2)]
        return remote(
            pair.at[pl.ds(start, CHUNK), :], pair.at[pl.ds(start + CHUNK, CHUNK), :],
            sib_send.at[u], sib_recv.at[u], sibling,
        )

    def share(d1, d2):
        u = UNIT[(d1, d2)]
        sib_copy(u, u % 2).start()

    send(0, 0, 0, 1, 1)
    send(0, 0, 1, 1, -1)
    share(0, 0)
    send(0, 0, 1, 1, 1)
    send(0, 0, 0, 1, -1)
    for copy in loads:
        copy.wait()

    for k in range(2):
        turned = rf[k]
        high = turned.astype(BF16)
        r2t[k, pl.ds(0, RANK), :] = high
        r2t[k, pl.ds(RANK, RANK), :] = (turned - high.astype(F32)).astype(BF16)

    def actions(step):
        if step == 0:
            arrived(3, 0, 0)
            arrived(1, 0, 1)
            send(3, 0, 0, 1, 1)
            send(1, 0, 1, 1, -1)
            send(0, 0, 0, 2, 1)
            send(0, 0, 1, 2, -1)
            send(0, 0, 1, 2, 1)
            send(0, 0, 0, 2, -1)
            send(3, 0, 0, 2, 1)
            send(1, 0, 1, 2, -1)
            send(1, 0, 1, 2, 1)
            send(3, 0, 0, 2, -1)
            arrived(3, 0, 1)
            arrived(1, 0, 0)
            share(3, 0)
            share(1, 0)
            arrived(0, 3, 0)
            arrived(0, 1, 1)
            send(0, 3, 0, 2, 1)
            send(0, 1, 1, 2, -1)
            send(3, 0, 1, 2, 1)
            send(1, 0, 0, 2, -1)
            send(1, 0, 0, 2, 1)
            send(3, 0, 1, 2, -1)
        if step == 1:
            arrived(0, 3, 1)
            arrived(0, 1, 0)
            share(0, 3)
            share(0, 1)
            arrived(2, 0, 0)
            arrived(2, 0, 1)
            send(2, 0, 0, 2, 1)
            send(2, 0, 1, 2, -1)
            share(2, 0)
        if step == 2:
            arrived(3, 3, 0)
            arrived(1, 1, 1)
            send(3, 3, 0, 2, 1)
            send(1, 1, 1, 2, -1)
            send(2, 0, 1, 2, 1)
            send(2, 0, 0, 2, -1)
        if step == 3:
            arrived(0, 2, 0)
            arrived(0, 2, 1)
            share(0, 2)
            arrived(3, 3, 1)
            arrived(1, 1, 0)
            share(3, 3)
            share(1, 1)
        if step == 4:
            arrived(1, 3, 0)
            arrived(3, 1, 1)
            send(1, 3, 0, 2, 1)
            send(3, 1, 1, 2, -1)
            arrived(1, 3, 1)
            arrived(3, 1, 0)
            share(1, 3)
            share(3, 1)
        if step == 5:
            arrived(2, 3, 0)
            arrived(2, 1, 1)
            send(2, 3, 0, 2, 1)
            send(2, 1, 1, 2, -1)
            arrived(2, 3, 1)
            arrived(2, 1, 0)
            share(2, 3)
            share(2, 1)
        if step == 6:
            arrived(3, 2, 0)
            arrived(1, 2, 1)
            arrived(3, 2, 1)
            arrived(1, 2, 0)
            share(3, 2)
            share(1, 2)
        if step == 7:
            arrived(2, 2, 0)
            arrived(2, 2, 1)
            share(2, 2)

    first_of = [d1 for d1, _ in ORDER]
    second_of = [d2 for _, d2 in ORDER]

    def cotangents(u):
        d1, d2 = pick(first_of, u), pick(second_of, u)
        other = t2 * lax.rem(p2 + d1, SIDE) + t1 * lax.rem(p1 + d2, SIDE) + (1 - c)
        return [
            up[:, pl.ds(pl.multiple_of(dev * CHUNK, CHUNK), CHUNK)]
            for dev in (plane(d1, d2), other)
        ]

    def pair_step(step, carry):
        for i in range(PAIRS):
            @pl.when(step == i)
            def _(i=i):
                actions(i)

        for half in range(2):
            sib_copy(2 * step + half, half).wait_recv()
        cot = jnp.concatenate(cotangents(2 * step) + cotangents(2 * step + 1), axis=1).astype(F32)
        rows = slots[step]
        pre = lax.dot_general(w[...], rows, NT, preferred_element_type=F32)
        gate_pre, up_pre = pre[:HID], pre[HID:]
        sig = jax.nn.sigmoid(gate_pre)
        grad_gate = (cot * up_pre * (sig * (1.0 + gate_pre * (1.0 - sig)))).astype(BF16)
        grad_up = (cot * (gate_pre * sig)).astype(BF16)
        grads = jnp.concatenate([grad_gate, grad_up], axis=0)
        acc[...] += jnp.dot(grads, rows, preferred_element_type=F32)
        return carry

    lax.fori_loop(0, PAIRS, pair_step, 0)
    pending = []

    def go(copy):
        copy.start()
        pending.append(copy)
        return copy

    def drain():
        for i, (d1, d2, h) in enumerate(started):
            remote(
                piece(d1, d2, h), piece(d1, d2, h), ag_send.at[i], ag_recv.at[0, 0], sibling
            ).wait_send()
        for u in range(UNITS):
            sib_copy(u, u % 2).wait_send()
        for copy in pending:
            copy.wait_send()
        store_delta.wait()
        store_left.wait()

    store_left = pltpu.make_async_copy(full, left_out, out_sem.at[1])
    store_delta = pltpu.make_async_copy(acc, delta_out, out_sem.at[0])
    store_delta.start()

    def left_part(k, g, dst):
        cols = pl.ds(512 * g, 512)
        block = acc[pl.ds(pl.multiple_of(HID * k, 32), HID), cols]
        high = block.astype(BF16)
        low = (block - high.astype(F32)).astype(BF16)
        dsplit[k, pl.ds(0, HID), cols] = high
        dsplit[k, pl.ds(HID, HID), cols] = low
        both = jnp.dot(r2t[k], high, preferred_element_type=F32)
        part = both[:RANK] + both[RANK:]
        part = part + jnp.dot(r2t[k, pl.ds(0, RANK), :], low, preferred_element_type=F32)
        for i in range(4):
            dst[4 * g + i] = part[:, 128 * i : 128 * (i + 1)]

    swaps = []
    for g in range(4):
        left_part(1 - c, g, snd_sib)
        group = pl.ds(4 * g, 4)
        swaps.append(
            go(remote(snd_sib.at[group], rcv_sib.at[group], a_send.at[g], a_recv.at[g], sibling))
        )
    for g in range(4):
        left_part(c, g, mine)
    for swap in swaps:
        swap.wait_recv()

    near_last = (2, 1, 3)
    near_first = (1, 3, 2)

    def group_at(q):
        return pl.ds(4 * q, 4)

    firsts = {}
    for off in near_last:
        q = lax.rem(p1 + off, SIDE)
        mine[group_at(q)] += rcv_sib[group_at(q)]
        firsts[off] = go(remote(
            mine.at[group_at(q)], recv1.at[off - 1],
            b_send.at[off - 1], b_recv.at[off - 1], first_peer(off),
        ))
    total = mine[group_at(p1)] + rcv_sib[group_at(p1)]
    for off in near_first:
        firsts[off].wait_recv()
        total = total + recv1[off - 1]
    s1[...] = total

    seconds = {}
    for off in near_last:
        seconds[off] = go(remote(
            s1.at[lax.rem(p2 + off, SIDE)], recv2.at[off - 1],
            c_send.at[off - 1], c_recv.at[off - 1], second_peer(off),
        ))
    total = s1[p2]
    for off in near_first:
        seconds[off].wait_recv()
        total = total + recv2[off - 1]
    s2[...] = total

    far_first = (4, 3, 5, 2, 6, 1, 7)
    far_last = far_first[::-1]

    def eight(i):
        return pl.ds(pl.multiple_of(8 * i, 8), 8)

    reps = {}
    for off in far_first:
        reps[off] = go(remote(
            s2.at[eight(lax.rem(z + off, REPS)), :], recv3.at[off - 1],
            z_send.at[off - 1], z_recv.at[off - 1], rep_peer(off),
        ))
    total = s2[eight(z), :]
    for off in far_last:
        reps[off].wait_recv()
        total = total + recv3[off - 1]

    whole[eight(z), :] = total * (1.0 / REPS)
    reps = {}
    for off in far_first:
        reps[off] = go(remote(
            whole.at[eight(z), :], whole.at[eight(z), :],
            gz_send.at[off - 1], gz_recv.at[off - 1], rep_peer(off),
        ))
    for off in far_last:
        reps[off].wait_recv()

    own_block = full.at[c, 4 * p1 + p2]
    own_block[...] = whole[...].astype(BF16)
    seconds = {}
    for off in near_last:
        seconds[off] = go(remote(
            own_block, own_block, gb_send.at[off - 1], gb_recv.at[off - 1], second_peer(off)
        ))
    for off in near_first:
        seconds[off].wait_recv()

    def pass_on(off):
        group = full.at[c, group_at(lax.rem(p1 + SIDE - off, SIDE))]
        return go(remote(group, group, gs_send.at[off], gs_recv.at[off], sibling))

    own_group = full.at[c, group_at(p1)]
    firsts = {}
    for off in near_last:
        firsts[off] = go(remote(
            own_group, own_group, gc_send.at[off - 1], gc_recv.at[off - 1], first_peer(off)
        ))
    passed = [pass_on(0)]
    for off in near_first:
        firsts[off].wait_recv()
        passed.append(pass_on(off))

    lane = lax.broadcasted_iota(jnp.int32, (RANK, 128), 1)
    row = lax.broadcasted_iota(jnp.int32, (RANK, 128), 0)

    def left_rows(k):
        return jnp.concatenate([full[k, i] for i in range(16)], axis=1)

    def product(k):
        left = left_rows(k)
        twice = jnp.concatenate([left, left], axis=0)
        part = lax.dot_general(dsplit[k], twice, NT, preferred_element_type=F32)
        return part[:HID] + part[HID:]

    prod_own = product(c)
    for copy in passed:
        copy.wait_recv()
    prod_other = product(1 - c)
    wide = lax.broadcasted_iota(jnp.int32, (HID, 128), 1)
    psum[pl.ds(0, HID), :] = jnp.where((wide < RANK) == (c == 0), prod_own, prod_other)
    psum[pl.ds(HID, 32), :] = jnp.zeros((32, 128), F32)

    def p_rows(i):
        return pl.ds(pl.multiple_of(32 * i, 32), 32)

    reps = {}
    for off in far_first:
        reps[off] = go(remote(
            psum.at[p_rows(lax.rem(z + off, REPS)), :], recv4.at[off - 1],
            pz_send.at[off - 1], pz_recv.at[off - 1], rep_peer(off),
        ))
    store_left.start()

    for k in range(2):
        left = left_rows(k)
        padded = jnp.concatenate([left, jnp.zeros_like(left)], axis=0)
        gram = lax.dot_general(left, padded, NT, preferred_element_type=F32)
        aug[k] = jnp.where(lane == row + RANK, 1.0, gram)

    def eliminate(j, carry):
        for k in range(2):
            table = aug[k]
            pivot_row = aug[k, pl.ds(j, 1), :]
            at_j = lane == j
            pivot = jnp.sum(jnp.where(at_j[:1], pivot_row, 0.0), axis=1, keepdims=True)
            column = jnp.sum(jnp.where(at_j, table, 0.0), axis=1, keepdims=True)
            inv = lax.rsqrt(pivot)
            scaled = pivot_row * inv
            factor = column * inv
            aug[k] = jnp.where(
                row > j, table - factor * scaled, jnp.where(row == j, scaled, table)
            )
        return carry

    lax.fori_loop(0, RANK // 2, eliminate, 0)

    total = psum[p_rows(z), :]
    for off in far_last:
        reps[off].wait_recv()
        total = total + recv4[off - 1]
    pfull[p_rows(z), :] = total * (1.0 / REPS)
    reps = {}
    for off in far_first:
        reps[off] = go(remote(
            pfull.at[p_rows(z), :], pfull.at[p_rows(z), :],
            pg_send.at[off - 1], pg_recv.at[off - 1], rep_peer(off),
        ))

    lax.fori_loop(RANK // 2, RANK, eliminate, 0)

    inverse0 = jnp.where(lane < RANK, pltpu.roll(aug[0], RANK, 1), 0.0)
    inverse1 = jnp.where(lane >= RANK, aug[1], 0.0)
    solve_out[pl.ds(0, RANK), :] = inverse0
    solve_out[pl.ds(RANK, RANK), :] = inverse1
    both = jnp.concatenate([inverse0, inverse1], axis=0)
    solve_out[pl.ds(2 * RANK, 2 * RANK), :] = jnp.dot(
        both.T, both, precision=highest, preferred_element_type=F32
    )

    for off in far_last:
        reps[off].wait_recv()
    p_out[...] = pfull[...]

    drain()


AG_SENDS = 30


def step_call(tokens, upstream, weight, feedback, right_factor):
    any_space = pl.BlockSpec(memory_space=pl.ANY)
    vmem = pl.BlockSpec(memory_space=pltpu.VMEM)
    dma = pltpu.SemaphoreType.DMA
    return pl.pallas_call(
        step_kernel,
        name="gather_reduce",
        out_shape=(
            jax.ShapeDtypeStruct((2 * HID, DIM), F32),
            jax.ShapeDtypeStruct((2, 16, RANK, 128), BF16),
            jax.ShapeDtypeStruct((256, 128), F32),
            jax.ShapeDtypeStruct((256, 128), F32),
        ),
        in_specs=[any_space] * 5,
        out_specs=(any_space, any_space, vmem, vmem),
        scratch_shapes=[
            pltpu.VMEM((PAIRS, 4 * CHUNK, DIM), BF16),
            pltpu.VMEM((2 * HID, DIM), F32),
            pltpu.VMEM((2 * HID, DIM), BF16),
            pltpu.VMEM((HID, 32 * CHUNK), BF16),
            pltpu.VMEM((2, RANK, HID), F32),
            pltpu.VMEM((2, 2 * RANK, HID), BF16),
            pltpu.VMEM((2, 2 * HID, DIM), BF16),
            pltpu.VMEM((16, RANK, 128), F32),
            pltpu.VMEM((16, RANK, 128), F32),
            pltpu.VMEM((16, RANK, 128), F32),
            pltpu.VMEM((3, 4, RANK, 128), F32),
            pltpu.VMEM((4, RANK, 128), F32),
            pltpu.VMEM((3, RANK, 128), F32),
            pltpu.VMEM((RANK, 128), F32),
            pltpu.VMEM((7, 8, 128), F32),
            pltpu.VMEM((RANK, 128), F32),
            pltpu.VMEM((2, 16, RANK, 128), BF16),
            pltpu.VMEM((256, 128), F32),
            pltpu.VMEM((7, 32, 128), F32),
            pltpu.VMEM((256, 128), F32),
            pltpu.VMEM((2, RANK, 128), F32),
            dma((5,)), dma((2,)),
            dma((AG_SENDS,)), dma((UNITS, 2)), dma((UNITS,)), dma((UNITS,)),
            dma((4,)), dma((4,)), dma((3,)), dma((3,)), dma((3,)), dma((3,)), dma((7,)), dma((7,)),
            dma((7,)), dma((7,)), dma((3,)), dma((3,)), dma((3,)), dma((3,)), dma((4,)), dma((4,)),
            dma((7,)), dma((7,)), dma((7,)), dma((7,)),
        ],
        compiler_params=pltpu.CompilerParams(
            collective_id=0, has_side_effects=True, vmem_limit_bytes=60 * 1024 * 1024
        ),
    )(
        tokens.reshape(CHUNK, DIM),
        upstream.reshape(HID, 32 * CHUNK),
        weight.reshape(2 * HID, DIM),
        feedback.reshape(2 * HID, DIM),
        jnp.swapaxes(right_factor, 1, 2),
    )


COLS = 256


def finish_kernel(
    z_ref, delta, left, solve, p, momentum, weight, fb_out, mom_out, w_out, right_out, coef
):
    j = pl.program_id(0)

    @pl.when(j == 0)
    def _():
        rows = p[pl.ds(0, HID), :]
        right = lax.dot_general(
            solve[pl.ds(0, 2 * RANK), :], rows, NT, precision=highest, preferred_element_type=F32
        )
        right_out[0] = right[:RANK]
        right_out[1] = right[RANK:]
        weights = lax.dot_general(
            rows, solve[pl.ds(2 * RANK, 2 * RANK), :], NT,
            precision=highest, preferred_element_type=F32,
        )
        lane = lax.broadcasted_iota(jnp.int32, (HID, 128), 1)
        for k in range(2):
            own = jnp.where((lane < RANK) == (k == 0), weights, 0.0)
            high = own.astype(BF16)
            coef[pl.ds(2 * k * HID, HID), :] = high
            coef[pl.ds((2 * k + 1) * HID, HID), :] = (own - high.astype(F32)).astype(BF16)

    block = jnp.concatenate(
        [jnp.concatenate([left[k, i] for i in range(COLS // 128)], axis=1) for k in range(2)], axis=0
    )
    terms = jnp.dot(coef[...], block, preferred_element_type=F32)
    for k in range(2):
        approx = terms[2 * k * HID : (2 * k + 1) * HID] + terms[(2 * k + 1) * HID : 2 * (k + 1) * HID]
        fb_out[k] = delta[k] - approx

        @pl.when(j == z_ref[0])
        def _(k=k, approx=approx):
            moved = momentum_decay * momentum[k] + approx
            mom_out[k] = moved
            w_out[k] = (weight[k].astype(F32) - step_rate * moved).astype(BF16)


def finish_call(slab, delta, left, solve, p, momentum, weight):
    whole = lambda *shape: pl.BlockSpec(shape, lambda j, s: (0,) * len(shape))
    return pl.pallas_call(
        finish_kernel,
        name="finish",
        grid_spec=pltpu.PrefetchScalarGridSpec(
            num_scalar_prefetch=1,
            grid=(DIM // COLS,),
            in_specs=[
                pl.BlockSpec((2, HID, COLS), lambda j, s: (0, 0, j)),
                pl.BlockSpec((2, COLS // 128, RANK, 128), lambda j, s: (0, j, 0, 0)),
                whole(256, 128),
                whole(256, 128),
                whole(2, HID, COLS),
                pl.BlockSpec((2, HID, COLS), lambda j, s: (0, 0, s[0])),
            ],
            out_specs=[
                pl.BlockSpec((2, HID, COLS), lambda j, s: (0, 0, j)),
                whole(2, HID, COLS),
                whole(2, HID, COLS),
                whole(2, RANK, HID),
            ],
            scratch_shapes=[pltpu.VMEM((4 * HID, 2 * RANK), BF16)],
        ),
        out_shape=(
            jax.ShapeDtypeStruct((2, HID, DIM), F32),
            jax.ShapeDtypeStruct((2, HID, COLS), F32),
            jax.ShapeDtypeStruct((2, HID, COLS), BF16),
            jax.ShapeDtypeStruct((2, RANK, HID), F32),
        ),
        compiler_params=pltpu.CompilerParams(dimension_semantics=("arbitrary",)),
    )(slab, delta, left, solve, p, momentum, weight)


def per_device(tokens, upstream, weight, feedback, momentum, right_factor):
    delta, left, solve, p = step_call(tokens, upstream, weight, feedback, right_factor)
    slab = lax.axis_index("rep").astype(jnp.int32).reshape(1)
    feedback_next, momentum_next, weight_next, right_next = finish_call(
        slab, delta.reshape(2, HID, DIM), left, solve, p, momentum, weight
    )
    return (feedback_next[None], momentum_next, weight_next, jnp.swapaxes(right_next, 1, 2))


def solution(mesh):
    placed = (
        P("rep", "fsdp", None),
        P("rep", "fsdp", None),
        P(None, "fsdp", None),
        P("rep", None, "fsdp", None),
        P(None, "fsdp", "rep"),
        P(None, "fsdp", None),
    )
    return jax.shard_map(
        per_device,
        mesh=mesh,
        in_specs=placed,
        out_specs=(
            P("rep", None, "fsdp", None),
            P(None, "fsdp", "rep"),
            P(None, "fsdp", "rep"),
            P(None, "fsdp", None),
        ),
        check_vma=False,
    )
```

time: 137 us -> 118 us (0.86)
  Pallas kernels: 133 us -> 117 us
  local copies, waits for them, and re-layouts: 3.44 us -> 0 us
    pallas_call x1, Pallas kernels: 121 us -> 109 us  [step_call(): pl.pallas_call(step_kernel, name='gather_reduce', out_shape=(jax.ShapeDty...]
    pallas_call x1, Pallas kernels: 12.3 us -> 8.44 us  [finish_call(): pl.pallas_call(finish_kernel, name='finish', grid_spec=pltpu.PrefetchScal...]
    unnamed x2 -> x0, local copies, waits for them, and re-layouts: 3.44 us -> none
where the time goes in v2:
time: 118 us
  Pallas kernels  117 us (99%)
    pallas_call x1, Pallas kernels, step_call(): pl.pallas_call(step_kernel, name='gather_reduce', out_shape=(jax.ShapeDty...  109 us
    pallas_call x1, Pallas kernels, finish_call(): pl.pallas_call(finish_kernel, name='finish', grid_spec=pltpu.PrefetchScal...  8.44 us

profile of v2, /device:TPU:1, one launch (start us, length us, event | category | flops | bytes accessed | tf_op | source)
XLA Modules:
  0.0 117.9 jit_solution(4793361516165815807)
XLA Ops:
  0.6 108.9 %gather_reduce.1 = (f32[448,2048]{1,0:T(8,128)}, bf16[2,16,64,128]{3,2,1,0:T(8,128)(2,1)}, f32[256,128]{1,0:T(8,128)}, f32[256,128]{1,0:T(8,128)}) custom-call(bf16[128,2048]{1,0:T(8,128)(2,1)} %bitcast.13, bf16[224,4096]{1,0:T(8,128)(2,1)} %bitcast.12, bf16[448,2048]{1,0:T(8,128)(2,1)} %bitcast.9, f32[448,2048]{1,0:T(8,128)} %bitcast.10, f32[2,64,224]{2,1,0:T(8,128)} %bitcast.14), custom_call_target="tpu_custom_call" | custom-call | tf_op jit(solution)/shard_map/gather_reduce/pallas_call | solution.py:497
  109.5 8.4 %finish.1 = (f32[2,224,2048]{2,1,0:T(8,128)}, f32[2,224,256]{2,1,0:T(8,128)}, bf16[2,224,256]{2,1,0:T(8,128)(2,1)}, f32[2,64,224]{2,1,0:T(8,128)}) custom-call(s32[1]{0:T(128)} %bitcast.z_ref, f32[2,224,2048]{2,1,0:T(8,128)} %bitcast.11, bf16[2,16,64,128]{3,2,1,0:T(8,128)(2,1)} %get-tuple-element.13.left, f32[256,128]{1,0:T(8,128)} %get-tuple-element.14.solve, ...), custom_call_target="tpu_custom_call" | custom-call | tf_op jit(solution)/shard_map/finish/pallas_call | solution.py:592

commit v3 on v2

--- a/solution.py
+++ b/solution.py
@@ -50,7 +50,7 @@
     tok_hbm, up_hbm, w_hbm, fb_hbm, rf_hbm,
     delta_out, left_out, solve_out, p_out,
     slots, acc, w, up, rf, r2t, dsplit,
-    snd_sib, rcv_sib, mine, recv1, s1, recv2, s2, recv3, whole, full, psum, recv4, pfull, aug,
+    snd_sib, rcv_sib, mine, recv1, s1, recv2, s2, recv3, whole, full, lsplit, psum, recv4, pfull,
     in_sem, out_sem, ag_send, ag_recv, sib_send, sib_recv,
     a_send, a_recv, b_send, b_recv, c_send, c_recv, z_send, z_recv,
     gz_send, gz_recv, gb_send, gb_recv, gc_send, gc_recv, gs_send, gs_recv,
@@ -177,15 +177,15 @@
             arrived(1, 0, 0)
             share(3, 0)
             share(1, 0)
-            arrived(0, 3, 0)
-            arrived(0, 1, 1)
-            send(0, 3, 0, 2, 1)
-            send(0, 1, 1, 2, -1)
             send(3, 0, 1, 2, 1)
             send(1, 0, 0, 2, -1)
             send(1, 0, 0, 2, 1)
             send(3, 0, 1, 2, -1)
         if step == 1:
+            arrived(0, 3, 0)
+            arrived(0, 1, 1)
+            send(0, 3, 0, 2, 1)
+            send(0, 1, 1, 2, -1)
             arrived(0, 3, 1)
             arrived(0, 1, 0)
             share(0, 3)
@@ -290,7 +290,7 @@
         store_delta.wait()
         store_left.wait()
 
-    store_left = pltpu.make_async_copy(full, left_out, out_sem.at[1])
+    store_left = pltpu.make_async_copy(lsplit, left_out, out_sem.at[1])
     store_delta = pltpu.make_async_copy(acc, delta_out, out_sem.at[0])
     store_delta.start()
 
@@ -321,23 +321,35 @@
 
     near_last = (2, 1, 3)
     near_first = (1, 3, 2)
-
-    def group_at(q):
-        return pl.ds(4 * q, 4)
-
-    firsts = {}
-    for off in near_last:
-        q = lax.rem(p1 + off, SIDE)
-        mine[group_at(q)] += rcv_sib[group_at(q)]
-        firsts[off] = go(remote(
-            mine.at[group_at(q)], recv1.at[off - 1],
-            b_send.at[off - 1], b_recv.at[off - 1], first_peer(off),
-        ))
-    total = mine[group_at(p1)] + rcv_sib[group_at(p1)]
-    for off in near_first:
-        firsts[off].wait_recv()
-        total = total + recv1[off - 1]
-    s1[...] = total
+    after, before = first_peer(1), first_peer(3)
+
+    def group_of(off, half):
+        return pl.ds(4 * lax.rem(p1 + off, SIDE) + 2 * half, 2)
+
+    def add_sibling(off):
+        group = pl.ds(4 * lax.rem(p1 + off, SIDE), 4)
+        mine[group] += rcv_sib[group]
+
+    def ring(group, slot, dev):
+        return go(remote(mine.at[group], recv1.at[slot], b_send.at[slot], b_recv.at[slot], dev))
+
+    add_sibling(2)
+    hops = [ring(group_of(2, 0), 0, after), ring(group_of(2, 1), 3, before)]
+    add_sibling(1)
+    hops.append(ring(group_of(1, 1), 1, after))
+    add_sibling(3)
+    hops.append(ring(group_of(3, 0), 4, before))
+    add_sibling(0)
+    hops[0].wait_recv()
+    mine[group_of(1, 0)] += recv1[0]
+    hops.append(ring(group_of(1, 0), 2, after))
+    hops[1].wait_recv()
+    mine[group_of(3, 1)] += recv1[3]
+    hops.append(ring(group_of(3, 1), 5, before))
+    for hop in hops[2:]:
+        hop.wait_recv()
+    s1[pl.ds(0, 2)] = mine[group_of(0, 0)] + recv1[2] + recv1[4]
+    s1[pl.ds(2, 2)] = mine[group_of(0, 1)] + recv1[1] + recv1[5]
 
     seconds = {}
     for off in near_last:
@@ -379,7 +391,7 @@
         reps[off].wait_recv()
 
     own_block = full.at[c, 4 * p1 + p2]
-    own_block[...] = whole[...].astype(BF16)
+    own_block[...] = whole[...]
     seconds = {}
     for off in near_last:
         seconds[off] = go(remote(
@@ -388,91 +400,119 @@
     for off in near_first:
         seconds[off].wait_recv()
 
-    def pass_on(off):
-        group = full.at[c, group_at(lax.rem(p1 + SIDE - off, SIDE))]
-        return go(remote(group, group, gs_send.at[off], gs_recv.at[off], sibling))
-
-    own_group = full.at[c, group_at(p1)]
-    firsts = {}
-    for off in near_last:
-        firsts[off] = go(remote(
-            own_group, own_group, gc_send.at[off - 1], gc_recv.at[off - 1], first_peer(off)
-        ))
-    passed = [pass_on(0)]
-    for off in near_first:
-        firsts[off].wait_recv()
-        passed.append(pass_on(off))
+    def spread(off, half, slot, dev):
+        group = full.at[c, group_of(off, half)]
+        return go(remote(group, group, gc_send.at[slot], gc_recv.at[slot], dev))
+
+    passed = []
+
+    def pass_on(off, half):
+        group = full.at[c, group_of(off, half)]
+        n = len(passed)
+        passed.append(go(remote(group, group, gs_send.at[n], gs_recv.at[n], sibling)))
+
+    hops = [
+        spread(0, 0, 0, after), spread(0, 1, 1, before),
+        spread(0, 1, 2, after), spread(0, 0, 3, before),
+    ]
+    pass_on(0, 0)
+    pass_on(0, 1)
+    hops[0].wait_recv()
+    hops.append(spread(3, 0, 4, after))
+    hops[1].wait_recv()
+    hops.append(spread(1, 1, 5, before))
+    pass_on(3, 0)
+    pass_on(1, 1)
+    hops[2].wait_recv()
+    pass_on(3, 1)
+    hops[3].wait_recv()
+    pass_on(1, 0)
+    hops[4].wait_recv()
+    pass_on(2, 0)
+    hops[5].wait_recv()
+    pass_on(2, 1)
 
     lane = lax.broadcasted_iota(jnp.int32, (RANK, 128), 1)
     row = lax.broadcasted_iota(jnp.int32, (RANK, 128), 0)
 
-    def left_rows(k):
-        return jnp.concatenate([full[k, i] for i in range(16)], axis=1)
+    def split_left(k):
+        left = jnp.concatenate([full[k, i] for i in range(16)], axis=1)
+        high = left.astype(BF16)
+        rows = pl.ds(pl.multiple_of(RANK * k, RANK), RANK)
+        lsplit[0, rows, :] = high
+        lsplit[1, rows, :] = (left - high.astype(F32)).astype(BF16)
+
+    def left_terms(k):
+        rows = pl.ds(pl.multiple_of(RANK * k, RANK), RANK)
+        return jnp.concatenate([lsplit[0, rows, :], lsplit[1, rows, :]], axis=0)
 
     def product(k):
-        left = left_rows(k)
-        twice = jnp.concatenate([left, left], axis=0)
-        part = lax.dot_general(dsplit[k], twice, NT, preferred_element_type=F32)
-        return part[:HID] + part[HID:]
-
-    prod_own = product(c)
+        part = lax.dot_general(dsplit[k], left_terms(k), NT, preferred_element_type=F32)
+        part = part[:HID] + part[HID:]
+        part = part + pltpu.roll(part, RANK, 1)
+        wide = lax.broadcasted_iota(jnp.int32, (HID // 2, 128), 1)
+        return jnp.where(wide < RANK, part[: HID // 2], part[HID // 2 :])
+
+    def p_rows(i):
+        return pl.ds(pl.multiple_of(16 * i, 16), 16)
+
+    def scatter(slot, k):
+        psum[slot, pl.ds(0, HID // 2), :] = product(k)
+        psum[slot, pl.ds(HID // 2, 16), :] = jnp.zeros((16, 128), F32)
+        out = {}
+        for off in far_first:
+            n = 7 * slot + off - 1
+            out[off] = go(remote(
+                psum.at[slot, p_rows(lax.rem(z + off, REPS)), :], recv4.at[slot, off - 1],
+                pz_send.at[n], pz_recv.at[n], rep_peer(off),
+            ))
+        return out
+
+    split_left(c)
+    parts = [scatter(0, c)]
     for copy in passed:
         copy.wait_recv()
-    prod_other = product(1 - c)
-    wide = lax.broadcasted_iota(jnp.int32, (HID, 128), 1)
-    psum[pl.ds(0, HID), :] = jnp.where((wide < RANK) == (c == 0), prod_own, prod_other)
-    psum[pl.ds(HID, 32), :] = jnp.zeros((32, 128), F32)
-
-    def p_rows(i):
-        return pl.ds(pl.multiple_of(32 * i, 32), 32)
-
+    split_left(1 - c)
+    parts.append(scatter(1, 1 - c))
+    store_left.start()
+
+    tables = []
+    for k in range(2):
+        terms = left_terms(k)
+        gram = lax.dot_general(terms, terms, NT, preferred_element_type=F32)
+        gram = gram[:RANK] + gram[RANK:]
+        gram = gram + pltpu.roll(gram, RANK, 1)
+        tables.append(jnp.where(lane < RANK, gram, jnp.where(lane == row + RANK, 1.0, 0.0)))
+
+    def eliminate(j):
+        for k in range(2):
+            table = tables[k]
+            inv = lax.rsqrt(table[j : j + 1, j : j + 1])
+            scaled = table[j : j + 1, :] * inv
+            factor = jnp.where(row[:, :1] > j, table[:, j : j + 1] * inv, 0.0)
+            tables[k] = jnp.where(row == j, scaled, table - factor * scaled)
+
+    for j in range(RANK // 2):
+        eliminate(j)
+
+    for slot in range(2):
+        total = psum[slot, p_rows(z), :]
+        for off in far_last:
+            parts[slot][off].wait_recv()
+            total = total + recv4[slot, off - 1]
+        pfull[slot, p_rows(z), :] = total * (1.0 / REPS)
     reps = {}
     for off in far_first:
         reps[off] = go(remote(
-            psum.at[p_rows(lax.rem(z + off, REPS)), :], recv4.at[off - 1],
-            pz_send.at[off - 1], pz_recv.at[off - 1], rep_peer(off),
-        ))
-    store_left.start()
-
-    for k in range(2):
-        left = left_rows(k)
-        padded = jnp.concatenate([left, jnp.zeros_like(left)], axis=0)
-        gram = lax.dot_general(left, padded, NT, preferred_element_type=F32)
-        aug[k] = jnp.where(lane == row + RANK, 1.0, gram)
-
-    def eliminate(j, carry):
-        for k in range(2):
-            table = aug[k]
-            pivot_row = aug[k, pl.ds(j, 1), :]
-            at_j = lane == j
-            pivot = jnp.sum(jnp.where(at_j[:1], pivot_row, 0.0), axis=1, keepdims=True)
-            column = jnp.sum(jnp.where(at_j, table, 0.0), axis=1, keepdims=True)
-            inv = lax.rsqrt(pivot)
-            scaled = pivot_row * inv
-            factor = column * inv
-            aug[k] = jnp.where(
-                row > j, table - factor * scaled, jnp.where(row == j, scaled, table)
-            )
-        return carry
-
-    lax.fori_loop(0, RANK // 2, eliminate, 0)
-
-    total = psum[p_rows(z), :]
-    for off in far_last:
-        reps[off].wait_recv()
-        total = total + recv4[off - 1]
-    pfull[p_rows(z), :] = total * (1.0 / REPS)
-    reps = {}
-    for off in far_first:
-        reps[off] = go(remote(
-            pfull.at[p_rows(z), :], pfull.at[p_rows(z), :],
+            pfull.at[:, p_rows(z), :], pfull.at[:, p_rows(z), :],
             pg_send.at[off - 1], pg_recv.at[off - 1], rep_peer(off),
         ))
 
-    lax.fori_loop(RANK // 2, RANK, eliminate, 0)
-
-    inverse0 = jnp.where(lane < RANK, pltpu.roll(aug[0], RANK, 1), 0.0)
-    inverse1 = jnp.where(lane >= RANK, aug[1], 0.0)
+    for j in range(RANK // 2, RANK):
+        eliminate(j)
+
+    inverse0 = jnp.where(lane < RANK, pltpu.roll(tables[0], RANK, 1), 0.0)
+    inverse1 = jnp.where(lane >= RANK, tables[1], 0.0)
     solve_out[pl.ds(0, RANK), :] = inverse0
     solve_out[pl.ds(RANK, RANK), :] = inverse1
     both = jnp.concatenate([inverse0, inverse1], axis=0)
@@ -482,7 +522,13 @@
 
     for off in far_last:
         reps[off].wait_recv()
-    p_out[...] = pfull[...]
+    own, other = pfull[0, pl.ds(0, HID // 2), :], pfull[1, pl.ds(0, HID // 2), :]
+    gate = jnp.where(c == 0, own, other)
+    gate = jnp.concatenate([gate, pltpu.roll(gate, RANK, 1)], axis=0)
+    raised = jnp.where(c == 0, other, own)
+    raised = jnp.concatenate([pltpu.roll(raised, RANK, 1), raised], axis=0)
+    wide = lax.broadcasted_iota(jnp.int32, (HID, 128), 1)
+    p_out[...] = jnp.where(wide < RANK, gate, raised)
 
     drain()
 
@@ -499,9 +545,9 @@
         name="gather_reduce",
         out_shape=(
             jax.ShapeDtypeStruct((2 * HID, DIM), F32),
-            jax.ShapeDtypeStruct((2, 16, RANK, 128), BF16),
+            jax.ShapeDtypeStruct((2, 2 * RANK, DIM), BF16),
             jax.ShapeDtypeStruct((256, 128), F32),
-            jax.ShapeDtypeStruct((256, 128), F32),
+            jax.ShapeDtypeStruct((HID, 128), F32),
         ),
         in_specs=[any_space] * 5,
         out_specs=(any_space, any_space, vmem, vmem),
@@ -516,22 +562,22 @@
             pltpu.VMEM((16, RANK, 128), F32),
             pltpu.VMEM((16, RANK, 128), F32),
             pltpu.VMEM((16, RANK, 128), F32),
-            pltpu.VMEM((3, 4, RANK, 128), F32),
+            pltpu.VMEM((6, 2, RANK, 128), F32),
             pltpu.VMEM((4, RANK, 128), F32),
             pltpu.VMEM((3, RANK, 128), F32),
             pltpu.VMEM((RANK, 128), F32),
             pltpu.VMEM((7, 8, 128), F32),
             pltpu.VMEM((RANK, 128), F32),
-            pltpu.VMEM((2, 16, RANK, 128), BF16),
-            pltpu.VMEM((256, 128), F32),
-            pltpu.VMEM((7, 32, 128), F32),
-            pltpu.VMEM((256, 128), F32),
-            pltpu.VMEM((2, RANK, 128), F32),
+            pltpu.VMEM((2, 16, RANK, 128), F32),
+            pltpu.VMEM((2, 2 * RANK, DIM), BF16),
+            pltpu.VMEM((2, 128, 128), F32),
+            pltpu.VMEM((2, 7, 16, 128), F32),
+            pltpu.VMEM((2, 128, 128), F32),
             dma((5,)), dma((2,)),
             dma((AG_SENDS,)), dma((UNITS, 2)), dma((UNITS,)), dma((UNITS,)),
-            dma((4,)), dma((4,)), dma((3,)), dma((3,)), dma((3,)), dma((3,)), dma((7,)), dma((7,)),
-            dma((7,)), dma((7,)), dma((3,)), dma((3,)), dma((3,)), dma((3,)), dma((4,)), dma((4,)),
-            dma((7,)), dma((7,)), dma((7,)), dma((7,)),
+            dma((4,)), dma((4,)), dma((6,)), dma((6,)), dma((3,)), dma((3,)), dma((7,)), dma((7,)),
+            dma((7,)), dma((7,)), dma((3,)), dma((3,)), dma((6,)), dma((6,)), dma((8,)), dma((8,)),
+            dma((14,)), dma((14,)), dma((7,)), dma((7,)),
         ],
         compiler_params=pltpu.CompilerParams(
             collective_id=0, has_side_effects=True, vmem_limit_bytes=60 * 1024 * 1024
@@ -545,87 +591,120 @@
     )
 
 
-COLS = 256
+COLS = 512
+SLAB = DIM // REPS
 
 
 def finish_kernel(
-    z_ref, delta, left, solve, p, momentum, weight, fb_out, mom_out, w_out, right_out, coef
+    delta_hbm, left_hbm, solve_hbm, p_hbm, mom_hbm, w_hbm, fb_out, mom_out, w_out, right_out,
+    delta, left, solve, p, mom, w, wnext, right, coef, in_sem, out_sem,
 ):
-    j = pl.program_id(0)
-
-    @pl.when(j == 0)
-    def _():
-        rows = p[pl.ds(0, HID), :]
-        right = lax.dot_general(
-            solve[pl.ds(0, 2 * RANK), :], rows, NT, precision=highest, preferred_element_type=F32
+    z = lax.axis_index("rep")
+    slab = pl.ds(pl.multiple_of(SLAB * z, SLAB), SLAB)
+    loads = [
+        pltpu.make_async_copy(solve_hbm, solve, in_sem.at[0]),
+        pltpu.make_async_copy(p_hbm, p, in_sem.at[1]),
+        pltpu.make_async_copy(left_hbm, left, in_sem.at[2]),
+    ]
+    chunks = [pl.ds(COLS * j, COLS) for j in range(DIM // COLS)]
+    for j, cols in enumerate(chunks):
+        loads.append(
+            pltpu.make_async_copy(delta_hbm.at[:, :, cols], delta.at[:, :, cols], in_sem.at[3 + j])
         )
-        right_out[0] = right[:RANK]
-        right_out[1] = right[RANK:]
-        weights = lax.dot_general(
-            rows, solve[pl.ds(2 * RANK, 2 * RANK), :], NT,
-            precision=highest, preferred_element_type=F32,
+    late = 3 + len(chunks)
+    loads.append(pltpu.make_async_copy(mom_hbm, mom, in_sem.at[late]))
+    loads.append(pltpu.make_async_copy(w_hbm.at[:, :, slab], w, in_sem.at[late + 1]))
+    for copy in loads:
+        copy.start()
+    loads[0].wait()
+    loads[1].wait()
+
+    rows = p[...]
+    weights = lax.dot_general(
+        rows, solve[pl.ds(2 * RANK, 2 * RANK), :], NT,
+        precision=highest, preferred_element_type=F32,
+    )
+    lane = lax.broadcasted_iota(jnp.int32, (HID, 128), 1)
+    for k in range(2):
+        own = jnp.where((lane < RANK) == (k == 0), weights, 0.0)
+        high = own.astype(BF16)
+        coef[pl.ds(k * HID, HID), :] = high
+        coef[pl.ds((2 + k) * HID, HID), :] = (own - high.astype(F32)).astype(BF16)
+    loads[2].wait()
+
+    def approx_at(cols):
+        terms = jnp.dot(coef[...], left[0, :, cols], preferred_element_type=F32)
+        more = jnp.dot(coef[pl.ds(0, 2 * HID), :], left[1, :, cols], preferred_element_type=F32)
+        return terms[: 2 * HID] + terms[2 * HID :] + more
+
+    stores = []
+    for j, cols in enumerate(chunks):
+        approx = approx_at(cols)
+        loads[3 + j].wait()
+        for k in range(2):
+            delta[k, :, cols] = delta[k, :, cols] - approx[k * HID : (k + 1) * HID]
+        stores.append(
+            pltpu.make_async_copy(delta.at[:, :, cols], fb_out.at[:, :, cols], out_sem.at[j])
         )
-        lane = lax.broadcasted_iota(jnp.int32, (HID, 128), 1)
-        for k in range(2):
-            own = jnp.where((lane < RANK) == (k == 0), weights, 0.0)
-            high = own.astype(BF16)
-            coef[pl.ds(2 * k * HID, HID), :] = high
-            coef[pl.ds((2 * k + 1) * HID, HID), :] = (own - high.astype(F32)).astype(BF16)
-
-    block = jnp.concatenate(
-        [jnp.concatenate([left[k, i] for i in range(COLS // 128)], axis=1) for k in range(2)], axis=0
+        stores[-1].start()
+
+    approx = approx_at(slab)
+    loads[late].wait()
+    loads[late + 1].wait()
+    for k in range(2):
+        moved = momentum_decay * mom[k] + approx[k * HID : (k + 1) * HID]
+        mom[k] = moved
+        wnext[k] = (w[k].astype(F32) - step_rate * moved).astype(BF16)
+    turned = lax.dot_general(
+        solve[pl.ds(0, 2 * RANK), :], rows, NT, precision=highest, preferred_element_type=F32
     )
-    terms = jnp.dot(coef[...], block, preferred_element_type=F32)
-    for k in range(2):
-        approx = terms[2 * k * HID : (2 * k + 1) * HID] + terms[(2 * k + 1) * HID : 2 * (k + 1) * HID]
-        fb_out[k] = delta[k] - approx
-
-        @pl.when(j == z_ref[0])
-        def _(k=k, approx=approx):
-            moved = momentum_decay * momentum[k] + approx
-            mom_out[k] = moved
-            w_out[k] = (weight[k].astype(F32) - step_rate * moved).astype(BF16)
-
-
-def finish_call(slab, delta, left, solve, p, momentum, weight):
-    whole = lambda *shape: pl.BlockSpec(shape, lambda j, s: (0,) * len(shape))
+    right[0] = turned[:RANK]
+    right[1] = turned[RANK:]
+    n = len(chunks)
+    stores.append(pltpu.make_async_copy(mom, mom_out, out_sem.at[n]))
+    stores.append(pltpu.make_async_copy(wnext, w_out, out_sem.at[n + 1]))
+    stores.append(pltpu.make_async_copy(right, right_out, out_sem.at[n + 2]))
+    for copy in stores[n:]:
+        copy.start()
+    for copy in stores:
+        copy.wait()
+
+
+def finish_call(delta, left, solve, p, momentum, weight):
+    any_space = pl.BlockSpec(memory_space=pl.ANY)
+    dma = pltpu.SemaphoreType.DMA
+    n = DIM // COLS
     return pl.pallas_call(
         finish_kernel,
         name="finish",
-        grid_spec=pltpu.PrefetchScalarGridSpec(
-            num_scalar_prefetch=1,
-            grid=(DIM // COLS,),
-            in_specs=[
-                pl.BlockSpec((2, HID, COLS), lambda j, s: (0, 0, j)),
-                pl.BlockSpec((2, COLS // 128, RANK, 128), lambda j, s: (0, j, 0, 0)),
-                whole(256, 128),
-                whole(256, 128),
-                whole(2, HID, COLS),
-                pl.BlockSpec((2, HID, COLS), lambda j, s: (0, 0, s[0])),
-            ],
-            out_specs=[
-                pl.BlockSpec((2, HID, COLS), lambda j, s: (0, 0, j)),
-                whole(2, HID, COLS),
-                whole(2, HID, COLS),
-                whole(2, RANK, HID),
-            ],
-            scratch_shapes=[pltpu.VMEM((4 * HID, 2 * RANK), BF16)],
-        ),
+        in_specs=[any_space] * 6,
+        out_specs=(any_space,) * 4,
         out_shape=(
             jax.ShapeDtypeStruct((2, HID, DIM), F32),
-            jax.ShapeDtypeStruct((2, HID, COLS), F32),
-            jax.ShapeDtypeStruct((2, HID, COLS), BF16),
+            jax.ShapeDtypeStruct((2, HID, SLAB), F32),
+            jax.ShapeDtypeStruct((2, HID, SLAB), BF16),
             jax.ShapeDtypeStruct((2, RANK, HID), F32),
         ),
-        compiler_params=pltpu.CompilerParams(dimension_semantics=("arbitrary",)),
-    )(slab, delta, left, solve, p, momentum, weight)
+        scratch_shapes=[
+            pltpu.VMEM((2, HID, DIM), F32),
+            pltpu.VMEM((2, 2 * RANK, DIM), BF16),
+            pltpu.VMEM((256, 128), F32),
+            pltpu.VMEM((HID, 128), F32),
+            pltpu.VMEM((2, HID, SLAB), F32),
+            pltpu.VMEM((2, HID, SLAB), BF16),
+            pltpu.VMEM((2, HID, SLAB), BF16),
+            pltpu.VMEM((2, RANK, HID), F32),
+            pltpu.VMEM((4 * HID, 2 * RANK), BF16),
+            dma((n + 5,)), dma((n + 3,)),
+        ],
+        compiler_params=pltpu.CompilerParams(vmem_limit_bytes=32 * 1024 * 1024),
+    )(delta, left, solve, p, momentum, weight)
 
 
 def per_device(tokens, upstream, weight, feedback, momentum, right_factor):
     delta, left, solve, p = step_call(tokens, upstream, weight, feedback, right_factor)
-    slab = lax.axis_index("rep").astype(jnp.int32).reshape(1)
     feedback_next, momentum_next, weight_next, right_next = finish_call(
-        slab, delta.reshape(2, HID, DIM), left, solve, p, momentum, weight
+        delta.reshape(2, HID, DIM), left, solve, p, momentum, weight
     )
     return (feedback_next[None], momentum_next, weight_next, jnp.swapaxes(right_next, 1, 2))
 

time: 118 us -> 124 us (1.051)
  local copies, waits for them, and re-layouts: 0 us -> 5.07 us
    unnamed x0 -> x12, local copies, waits for them, and re-layouts: none -> 5.07 us
    pallas_call x1, Pallas kernels: 8.44 us -> 5.66 us  [finish_call(): pl.pallas_call(finish_kernel, name='finish', in_specs=[any_space] * 6, ou...]
    pallas_call x1, Pallas kernels: 109 us -> 112 us  [step_call(): pl.pallas_call(step_kernel, name='gather_reduce', out_shape=(jax.ShapeDty...]
where the time goes in v3:
time: 124 us; the launch traced here: 123 us
  Pallas kernels  117 us (94%)
  local copies, waits for them, and re-layouts  5.07 us (4%)
    pallas_call x1, Pallas kernels, step_call(): pl.pallas_call(step_kernel, name='gather_reduce', out_shape=(jax.ShapeDty...  112 us
    pallas_call x1, Pallas kernels, finish_call(): pl.pallas_call(finish_kernel, name='finish', in_specs=[any_space] * 6, ou...  5.66 us
    unnamed x12, local copies, waits for them, and re-layouts  5.07 us

profile of v3, /device:TPU:1, one launch (start us, length us, event | category | flops | bytes accessed | tf_op | source)
XLA Modules:
  0.0 123.0 jit_solution(6340767045408520273)
XLA Ops:
  0.6 0.0 copy-start
  0.6 0.0 copy-start.3
  0.7 111.6 %gather_reduce.1 = (f32[448,2048]{1,0:T(8,128)}, bf16[2,128,2048]{2,1,0:T(8,128)(2,1)}, f32[256,128]{1,0:T(8,128)}, f32[224,128]{1,0:T(8,128)}) custom-call(bf16[128,2048]{1,0:T(8,128)(2,1)} %bitcast.12, bf16[224,4096]{1,0:T(8,128)(2,1)} %bitcast.11, bf16[448,2048]{1,0:T(8,128)(2,1)} %bitcast.8, f32[448,2048]{1,0:T(8,128)} %bitcast.10, f32[2,64,224]{2,1,0:T(8,128)} %bitcast.13), custom_call_target="tpu_custom_call" | custom-call | tf_op jit(solution)/shard_map/gather_reduce/pallas_call | solution.py:543
  112.3 0.0 copy-done
  112.3 0.0 copy-done.3
  112.3 0.0 copy-start.1
  112.3 2.0 %copy-done.1 = f32[448,2048]{1,0:T(8,128)S(1)} copy-done((f32[448,2048]{1,0:T(8,128)S(1)}, f32[448,2048]{1,0:T(8,128)}, u32[]{:S(2)}) %copy-start.1) | copy-done | bytes 3670040
  114.3 0.0 copy-start.2
  114.3 1.2 copy-done.2
  115.6 0.0 copy-start.4
  115.6 0.9 copy-done.4
  116.5 0.0 copy-start.5
  116.5 0.9 copy-done.5
  117.4 5.7 %finish.1 = (f32[2,224,2048]{2,1,0:T(8,128)}, f32[2,224,256]{2,1,0:T(8,128)}, bf16[2,224,256]{2,1,0:T(8,128)(2,1)}, f32[2,64,224]{2,1,0:T(8,128)}) custom-call(f32[2,224,2048]{2,1,0:T(8,128)S(1)} %bitcast.9, bf16[2,128,2048]{2,1,0:T(8,128)(2,1)S(1)} %copy-done.2, f32[256,128]{1,0:T(8,128)S(1)} %copy-done.4, f32[224,128]{1,0:T(8,128)S(1)} %copy-done.5, ...), custom_call_target="tpu_custom_call" | custom-call | tf_op jit(solution)/shard_map/finish/pallas_call | solution.py:677
Async XLA Ops:
  0.6 111.6 %copy-start = (bf16[2,224,2048]{2,1,0:T(8,128)(2,1)S(1)}, bf16[2,224,2048]{2,1,0:T(8,128)(2,1)}, u32[]{:S(2)}) copy-start(bf16[2,224,2048]{2,1,0:T(8,128)(2,1)} %w_hbm.1) | copy-start | bytes 5505028
  0.6 111.6 %copy-start.3 = (f32[2,224,256]{2,1,0:T(8,128)S(1)}, f32[2,224,256]{2,1,0:T(8,128)}, u32[]{:S(2)}) copy-start(f32[2,224,256]{2,1,0:T(8,128)} %mom_hbm.1) | copy-start | bytes 1376260
  112.3 2.0 %copy-start.1 = (f32[448,2048]{1,0:T(8,128)S(1)}, f32[448,2048]{1,0:T(8,128)}, u32[]{:S(2)}) copy-start(f32[448,2048]{1,0:T(8,128)} %get-tuple-element.12) | copy-start | bytes 11010052
  114.3 1.2 copy-start.2
  115.6 0.9 copy-start.4
  116.5 0.9 copy-start.5

commit v4 on v3

--- a/solution.py
+++ b/solution.py
@@ -54,7 +54,7 @@
     in_sem, out_sem, ag_send, ag_recv, sib_send, sib_recv,
     a_send, a_recv, b_send, b_recv, c_send, c_recv, z_send, z_recv,
     gz_send, gz_recv, gb_send, gb_recv, gc_send, gc_recv, gs_send, gs_recv,
-    pz_send, pz_recv, pg_send, pg_recv,
+    pz_send, pz_recv, pg_send, pg_recv, meet_sem,
 ):
     f = lax.axis_index("fsdp")
     z = lax.axis_index("rep")
@@ -98,14 +98,19 @@
         copy.start()
 
     barrier = pltpu.get_barrier_semaphore()
-    peers = [sibling]
-    peers += [first_peer(o) for o in (1, 2, 3)]
-    peers += [second_peer(o) for o in (1, 2, 3)]
-    peers += [rep_peer(o) for o in range(1, REPS)]
+    peers = [sibling, first_peer(1), first_peer(3), second_peer(1), second_peer(3)]
+    peers += [rep_peer(1), rep_peer(REPS - 1)]
+
+    def meet(turn, off):
+        for way in (off, REPS - off):
+            pl.semaphore_signal(
+                meet_sem.at[turn], inc=1, device_id=rep_peer(way), device_id_type=MESH
+            )
+
     for dev in peers:
         pl.semaphore_signal(barrier, inc=1, device_id=dev, device_id_type=MESH)
-    load_tok.wait()
     pl.semaphore_wait(barrier, len(peers))
+    meet(0, 1)
 
     started = []
 
@@ -120,8 +125,9 @@
         else:
             r1, r2 = d1, (d2 - way) % SIDE
             dev = second_peer(way % SIDE)
+        own = d1 == 0 and d2 == 0
         copy = remote(
-            piece(d1, d2, h), piece(r1, r2, h),
+            tok_hbm.at[pl.ds(HALF * h, HALF), :] if own else piece(d1, d2, h), piece(r1, r2, h),
             ag_send.at[len(started)], ag_recv.at[UNIT[(r1, r2)], h], dev,
         )
         copy.start()
@@ -145,11 +151,17 @@
         u = UNIT[(d1, d2)]
         sib_copy(u, u % 2).start()
 
+    def share_own():
+        remote(
+            tok_hbm, slots.at[0, pl.ds(CHUNK, CHUNK), :], sib_send.at[0], sib_recv.at[0], sibling
+        ).start()
+
     send(0, 0, 0, 1, 1)
     send(0, 0, 1, 1, -1)
-    share(0, 0)
+    share_own()
     send(0, 0, 1, 1, 1)
     send(0, 0, 0, 1, -1)
+    load_tok.wait()
     for copy in loads:
         copy.wait()
 
@@ -202,6 +214,8 @@
             send(1, 1, 1, 2, -1)
             send(2, 0, 1, 2, 1)
             send(2, 0, 0, 2, -1)
+            pl.semaphore_wait(meet_sem.at[0], 2)
+            meet(1, 2)
         if step == 3:
             arrived(0, 2, 0)
             arrived(0, 2, 1)
@@ -228,6 +242,7 @@
             arrived(2, 1, 0)
             share(2, 3)
             share(2, 1)
+            pl.semaphore_wait(meet_sem.at[1], 2)
         if step == 6:
             arrived(3, 2, 0)
             arrived(1, 2, 1)
@@ -400,37 +415,20 @@
     for off in near_first:
         seconds[off].wait_recv()
 
-    def spread(off, half, slot, dev):
-        group = full.at[c, group_of(off, half)]
-        return go(remote(group, group, gc_send.at[slot], gc_recv.at[slot], dev))
-
-    passed = []
-
-    def pass_on(off, half):
-        group = full.at[c, group_of(off, half)]
-        n = len(passed)
-        passed.append(go(remote(group, group, gs_send.at[n], gs_recv.at[n], sibling)))
-
-    hops = [
-        spread(0, 0, 0, after), spread(0, 1, 1, before),
-        spread(0, 1, 2, after), spread(0, 0, 3, before),
-    ]
-    pass_on(0, 0)
-    pass_on(0, 1)
-    hops[0].wait_recv()
-    hops.append(spread(3, 0, 4, after))
-    hops[1].wait_recv()
-    hops.append(spread(1, 1, 5, before))
-    pass_on(3, 0)
-    pass_on(1, 1)
-    hops[2].wait_recv()
-    pass_on(3, 1)
-    hops[3].wait_recv()
-    pass_on(1, 0)
-    hops[4].wait_recv()
-    pass_on(2, 0)
-    hops[5].wait_recv()
-    pass_on(2, 1)
+    def pass_on(off):
+        group = full.at[c, pl.ds(4 * lax.rem(p1 + SIDE - off, SIDE), 4)]
+        return go(remote(group, group, gs_send.at[off], gs_recv.at[off], sibling))
+
+    own_group = full.at[c, pl.ds(4 * p1, 4)]
+    firsts = {}
+    for off in near_last:
+        firsts[off] = go(remote(
+            own_group, own_group, gc_send.at[off - 1], gc_recv.at[off - 1], first_peer(off)
+        ))
+    passed = [pass_on(0)]
+    for off in near_first:
+        firsts[off].wait_recv()
+        passed.append(pass_on(off))
 
     lane = lax.broadcasted_iota(jnp.int32, (RANK, 128), 1)
     row = lax.broadcasted_iota(jnp.int32, (RANK, 128), 0)
@@ -576,8 +574,8 @@
             dma((5,)), dma((2,)),
             dma((AG_SENDS,)), dma((UNITS, 2)), dma((UNITS,)), dma((UNITS,)),
             dma((4,)), dma((4,)), dma((6,)), dma((6,)), dma((3,)), dma((3,)), dma((7,)), dma((7,)),
-            dma((7,)), dma((7,)), dma((3,)), dma((3,)), dma((6,)), dma((6,)), dma((8,)), dma((8,)),
-            dma((14,)), dma((14,)), dma((7,)), dma((7,)),
+            dma((7,)), dma((7,)), dma((3,)), dma((3,)), dma((3,)), dma((3,)), dma((4,)), dma((4,)),
+            dma((14,)), dma((14,)), dma((7,)), dma((7,)), pltpu.SemaphoreType.REGULAR((2,)),
         ],
         compiler_params=pltpu.CompilerParams(
             collective_id=0, has_side_effects=True, vmem_limit_bytes=60 * 1024 * 1024
@@ -604,14 +602,17 @@
     loads = [
         pltpu.make_async_copy(solve_hbm, solve, in_sem.at[0]),
         pltpu.make_async_copy(p_hbm, p, in_sem.at[1]),
-        pltpu.make_async_copy(left_hbm, left, in_sem.at[2]),
+    ]
+    loads += [
+        pltpu.make_async_copy(left_hbm.at[t], left.at[pl.ds(2 * RANK * i, 2 * RANK)], in_sem.at[2 + i])
+        for i, t in enumerate((0, 1, 0))
     ]
     chunks = [pl.ds(COLS * j, COLS) for j in range(DIM // COLS)]
     for j, cols in enumerate(chunks):
         loads.append(
-            pltpu.make_async_copy(delta_hbm.at[:, :, cols], delta.at[:, :, cols], in_sem.at[3 + j])
+            pltpu.make_async_copy(delta_hbm.at[:, :, cols], delta.at[:, :, cols], in_sem.at[5 + j])
         )
-    late = 3 + len(chunks)
+    late = 5 + len(chunks)
     loads.append(pltpu.make_async_copy(mom_hbm, mom, in_sem.at[late]))
     loads.append(pltpu.make_async_copy(w_hbm.at[:, :, slab], w, in_sem.at[late + 1]))
     for copy in loads:
@@ -628,19 +629,18 @@
     for k in range(2):
         own = jnp.where((lane < RANK) == (k == 0), weights, 0.0)
         high = own.astype(BF16)
-        coef[pl.ds(k * HID, HID), :] = high
-        coef[pl.ds((2 + k) * HID, HID), :] = (own - high.astype(F32)).astype(BF16)
-    loads[2].wait()
+        low = (own - high.astype(F32)).astype(BF16)
+        coef[pl.ds(k * HID, HID), :] = jnp.concatenate([high, high, low], axis=1)
+    for copy in loads[2:5]:
+        copy.wait()
 
     def approx_at(cols):
-        terms = jnp.dot(coef[...], left[0, :, cols], preferred_element_type=F32)
-        more = jnp.dot(coef[pl.ds(0, 2 * HID), :], left[1, :, cols], preferred_element_type=F32)
-        return terms[: 2 * HID] + terms[2 * HID :] + more
+        return jnp.dot(coef[...], left[:, cols], preferred_element_type=F32)
 
     stores = []
     for j, cols in enumerate(chunks):
         approx = approx_at(cols)
-        loads[3 + j].wait()
+        loads[5 + j].wait()
         for k in range(2):
             delta[k, :, cols] = delta[k, :, cols] - approx[k * HID : (k + 1) * HID]
         stores.append(
@@ -687,17 +687,17 @@
         ),
         scratch_shapes=[
             pltpu.VMEM((2, HID, DIM), F32),
-            pltpu.VMEM((2, 2 * RANK, DIM), BF16),
+            pltpu.VMEM((6 * RANK, DIM), BF16),
             pltpu.VMEM((256, 128), F32),
             pltpu.VMEM((HID, 128), F32),
             pltpu.VMEM((2, HID, SLAB), F32),
             pltpu.VMEM((2, HID, SLAB), BF16),
             pltpu.VMEM((2, HID, SLAB), BF16),
             pltpu.VMEM((2, RANK, HID), F32),
-            pltpu.VMEM((4 * HID, 2 * RANK), BF16),
-            dma((n + 5,)), dma((n + 3,)),
+            pltpu.VMEM((2 * HID, 6 * RANK), BF16),
+            dma((n + 7,)), dma((n + 3,)),
         ],
-        compiler_params=pltpu.CompilerParams(vmem_limit_bytes=32 * 1024 * 1024),
+        compiler_params=pltpu.CompilerParams(vmem_limit_bytes=60 * 1024 * 1024),
     )(delta, left, solve, p, momentum, weight)
 
 

time: 124 us -> 117 us (0.944)
  local copies, waits for them, and re-layouts: 5.07 us -> 0 us
    unnamed x12 -> x0, local copies, waits for them, and re-layouts: 5.07 us -> none
where the time goes in v4:
time: 117 us
  Pallas kernels  116 us (99%)
    pallas_call x1, Pallas kernels, step_call(): pl.pallas_call(step_kernel, name='gather_reduce', out_shape=(jax.ShapeDty...  111 us
    pallas_call x1, Pallas kernels, finish_call(): pl.pallas_call(finish_kernel, name='finish', in_specs=[any_space] * 6, ou...  5.5 us

profile of v4, /device:TPU:1, one launch (start us, length us, event | category | flops | bytes accessed | tf_op | source)
XLA Modules:
  0.0 117.0 jit_solution(7296459449865309950)
XLA Ops:
  0.6 110.9 %gather_reduce.1 = (f32[448,2048]{1,0:T(8,128)}, bf16[2,128,2048]{2,1,0:T(8,128)(2,1)}, f32[256,128]{1,0:T(8,128)}, f32[224,128]{1,0:T(8,128)}) custom-call(bf16[128,2048]{1,0:T(8,128)(2,1)} %bitcast.12, bf16[224,4096]{1,0:T(8,128)(2,1)} %bitcast.11, bf16[448,2048]{1,0:T(8,128)(2,1)} %bitcast.8, f32[448,2048]{1,0:T(8,128)} %bitcast.10, f32[2,64,224]{2,1,0:T(8,128)} %bitcast.13), custom_call_target="tpu_custom_call" | custom-call | tf_op jit(solution)/shard_map/gather_reduce/pallas_call | solution.py:541
  111.5 5.5 %finish.1 = (f32[2,224,2048]{2,1,0:T(8,128)}, f32[2,224,256]{2,1,0:T(8,128)}, bf16[2,224,256]{2,1,0:T(8,128)(2,1)}, f32[2,64,224]{2,1,0:T(8,128)}) custom-call(f32[2,224,2048]{2,1,0:T(8,128)} %bitcast.9, bf16[2,128,2048]{2,1,0:T(8,128)(2,1)} %get-tuple-element.13.left_hbm, f32[256,128]{1,0:T(8,128)} %get-tuple-element.14.solve_hbm, ...), custom_call_target="tpu_custom_call" | custom-call | tf_op jit(solution)/shard_map/finish/pallas_call | solution.py:677

commit v5 on v4

--- a/solution.py
+++ b/solution.py
@@ -310,7 +310,7 @@
     store_delta.start()
 
     def left_part(k, g, dst):
-        cols = pl.ds(512 * g, 512)
+        cols = pl.ds(pl.multiple_of(512 * g, 512), 512)
         block = acc[pl.ds(pl.multiple_of(HID * k, 32), HID), cols]
         high = block.astype(BF16)
         low = (block - high.astype(F32)).astype(BF16)
@@ -322,27 +322,27 @@
         for i in range(4):
             dst[4 * g + i] = part[:, 128 * i : 128 * (i + 1)]
 
-    swaps = []
-    for g in range(4):
+    near_last = (2, 1, 3)
+    near_first = (1, 3, 2)
+    swaps = {}
+    for n, off in enumerate(near_last + (0,)):
+        g = lax.rem(p2 + off, SIDE)
         left_part(1 - c, g, snd_sib)
         group = pl.ds(4 * g, 4)
-        swaps.append(
-            go(remote(snd_sib.at[group], rcv_sib.at[group], a_send.at[g], a_recv.at[g], sibling))
+        swaps[off] = go(
+            remote(snd_sib.at[group], rcv_sib.at[group], a_send.at[n], a_recv.at[n], sibling)
         )
-    for g in range(4):
-        left_part(c, g, mine)
-    for swap in swaps:
-        swap.wait_recv()
-
-    near_last = (2, 1, 3)
-    near_first = (1, 3, 2)
+
     after, before = first_peer(1), first_peer(3)
 
     def group_of(off, half):
         return pl.ds(4 * lax.rem(p1 + off, SIDE) + 2 * half, 2)
 
     def add_sibling(off):
-        group = pl.ds(4 * lax.rem(p1 + off, SIDE), 4)
+        q = lax.rem(p1 + off, SIDE)
+        left_part(c, q, mine)
+        swaps[off].wait_recv()
+        group = pl.ds(4 * q, 4)
         mine[group] += rcv_sib[group]
 
     def ring(group, slot, dev):
@@ -419,34 +419,47 @@
         group = full.at[c, pl.ds(4 * lax.rem(p1 + SIDE - off, SIDE), 4)]
         return go(remote(group, group, gs_send.at[off], gs_recv.at[off], sibling))
 
+    lane = lax.broadcasted_iota(jnp.int32, (RANK, 128), 1)
+    row = lax.broadcasted_iota(jnp.int32, (RANK, 128), 0)
+
+    def absorb(k, q):
+        left = jnp.concatenate([full[k, 4 * q + i] for i in range(4)], axis=1)
+        high = left.astype(BF16)
+        low = (left - high.astype(F32)).astype(BF16)
+        rows = pl.ds(pl.multiple_of(RANK * k, RANK), RANK)
+        cols = pl.ds(pl.multiple_of(512 * q, 512), 512)
+        lsplit[0, rows, cols] = high
+        lsplit[1, rows, cols] = low
+        terms = jnp.concatenate([high, low], axis=0)
+        part = lax.dot_general(dsplit[k, :, cols], terms, NT, preferred_element_type=F32)
+        return part[:HID] + part[HID:]
+
+    def absorb_own(off):
+        return absorb(c, lax.rem(p1 + SIDE - off, SIDE))
+
+    def absorb_other(off):
+        passed[off].wait_recv()
+        return absorb(1 - c, lax.rem(p2 + SIDE - off, SIDE))
+
     own_group = full.at[c, pl.ds(4 * p1, 4)]
     firsts = {}
     for off in near_last:
         firsts[off] = go(remote(
             own_group, own_group, gc_send.at[off - 1], gc_recv.at[off - 1], first_peer(off)
         ))
-    passed = [pass_on(0)]
+    passed = {0: pass_on(0)}
+    prod_own = absorb_own(0)
+    prod_other = absorb_other(0)
     for off in near_first:
         firsts[off].wait_recv()
-        passed.append(pass_on(off))
-
-    lane = lax.broadcasted_iota(jnp.int32, (RANK, 128), 1)
-    row = lax.broadcasted_iota(jnp.int32, (RANK, 128), 0)
-
-    def split_left(k):
-        left = jnp.concatenate([full[k, i] for i in range(16)], axis=1)
-        high = left.astype(BF16)
-        rows = pl.ds(pl.multiple_of(RANK * k, RANK), RANK)
-        lsplit[0, rows, :] = high
-        lsplit[1, rows, :] = (left - high.astype(F32)).astype(BF16)
+        passed[off] = pass_on(off)
+        prod_own = prod_own + absorb_own(off)
 
     def left_terms(k):
-        rows = pl.ds(pl.multiple_of(RANK * k, RANK), RANK)
+        rows = pl.ds(RANK * k, RANK)
         return jnp.concatenate([lsplit[0, rows, :], lsplit[1, rows, :]], axis=0)
 
-    def product(k):
-        part = lax.dot_general(dsplit[k], left_terms(k), NT, preferred_element_type=F32)
-        part = part[:HID] + part[HID:]
+    def packed(part):
         part = part + pltpu.roll(part, RANK, 1)
         wide = lax.broadcasted_iota(jnp.int32, (HID // 2, 128), 1)
         return jnp.where(wide < RANK, part[: HID // 2], part[HID // 2 :])
@@ -454,8 +467,8 @@
     def p_rows(i):
         return pl.ds(pl.multiple_of(16 * i, 16), 16)
 
-    def scatter(slot, k):
-        psum[slot, pl.ds(0, HID // 2), :] = product(k)
+    def scatter(slot, part):
+        psum[slot, pl.ds(0, HID // 2), :] = packed(part)
         psum[slot, pl.ds(HID // 2, 16), :] = jnp.zeros((16, 128), F32)
         out = {}
         for off in far_first:
@@ -466,12 +479,10 @@
             ))
         return out
 
-    split_left(c)
-    parts = [scatter(0, c)]
-    for copy in passed:
-        copy.wait_recv()
-    split_left(1 - c)
-    parts.append(scatter(1, 1 - c))
+    parts = [scatter(0, prod_own)]
+    for off in near_first:
+        prod_other = prod_other + absorb_other(off)
+    parts.append(scatter(1, prod_other))
     store_left.start()
 
     tables = []
@@ -638,34 +649,34 @@
         return jnp.dot(coef[...], left[:, cols], preferred_element_type=F32)
 
     stores = []
+
+    def store(src, dst):
+        stores.append(pltpu.make_async_copy(src, dst, out_sem.at[len(stores)]))
+        stores[-1].start()
+
     for j, cols in enumerate(chunks):
         approx = approx_at(cols)
         loads[5 + j].wait()
         for k in range(2):
             delta[k, :, cols] = delta[k, :, cols] - approx[k * HID : (k + 1) * HID]
-        stores.append(
-            pltpu.make_async_copy(delta.at[:, :, cols], fb_out.at[:, :, cols], out_sem.at[j])
-        )
-        stores[-1].start()
-
-    approx = approx_at(slab)
-    loads[late].wait()
-    loads[late + 1].wait()
-    for k in range(2):
-        moved = momentum_decay * mom[k] + approx[k * HID : (k + 1) * HID]
-        mom[k] = moved
-        wnext[k] = (w[k].astype(F32) - step_rate * moved).astype(BF16)
-    turned = lax.dot_general(
-        solve[pl.ds(0, 2 * RANK), :], rows, NT, precision=highest, preferred_element_type=F32
-    )
-    right[0] = turned[:RANK]
-    right[1] = turned[RANK:]
-    n = len(chunks)
-    stores.append(pltpu.make_async_copy(mom, mom_out, out_sem.at[n]))
-    stores.append(pltpu.make_async_copy(wnext, w_out, out_sem.at[n + 1]))
-    stores.append(pltpu.make_async_copy(right, right_out, out_sem.at[n + 2]))
-    for copy in stores[n:]:
-        copy.start()
+        store(delta.at[:, :, cols], fb_out.at[:, :, cols])
+        if j == 0:
+            turned = lax.dot_general(
+                solve[pl.ds(0, 2 * RANK), :], rows, NT,
+                precision=highest, preferred_element_type=F32,
+            )
+            right[0] = turned[:RANK]
+            right[1] = turned[RANK:]
+            store(right, right_out)
+            approx = approx_at(slab)
+            loads[late].wait()
+            loads[late + 1].wait()
+            for k in range(2):
+                moved = momentum_decay * mom[k] + approx[k * HID : (k + 1) * HID]
+                mom[k] = moved
+                wnext[k] = (w[k].astype(F32) - step_rate * moved).astype(BF16)
+            store(mom, mom_out)
+            store(wnext, w_out)
     for copy in stores:
         copy.wait()
 

time: 117 us -> 115 us (0.983)
    pallas_call x1, Pallas kernels: 111 us -> 109 us  [step_call(): pl.pallas_call(step_kernel, name='gather_reduce', out_shape=(jax.ShapeDty...]
where the time goes in v5:
time: 115 us
  Pallas kernels  115 us (100%)
    pallas_call x1, Pallas kernels, step_call(): pl.pallas_call(step_kernel, name='gather_reduce', out_shape=(jax.ShapeDty...  109 us
    pallas_call x1, Pallas kernels, finish_call(): pl.pallas_call(finish_kernel, name='finish', in_specs=[any_space] * 6, ou...  5.5 us

profile of v5, /device:TPU:1, one launch (start us, length us, event | category | flops | bytes accessed | tf_op | source)
XLA Modules:
  0.0 115.3 jit_solution(8067659590494852810)
XLA Ops:
  0.6 109.2 %gather_reduce.1 = (f32[448,2048]{1,0:T(8,128)}, bf16[2,128,2048]{2,1,0:T(8,128)(2,1)}, f32[256,128]{1,0:T(8,128)}, f32[224,128]{1,0:T(8,128)}) custom-call(bf16[128,2048]{1,0:T(8,128)(2,1)} %bitcast.12, bf16[224,4096]{1,0:T(8,128)(2,1)} %bitcast.11, bf16[448,2048]{1,0:T(8,128)(2,1)} %bitcast.8, f32[448,2048]{1,0:T(8,128)} %bitcast.10, f32[2,64,224]{2,1,0:T(8,128)} %bitcast.13), custom_call_target="tpu_custom_call" | custom-call | tf_op jit(solution)/shard_map/gather_reduce/pallas_call | solution.py:552
  109.8 5.5 %finish.1 = (f32[2,224,2048]{2,1,0:T(8,128)}, f32[2,224,256]{2,1,0:T(8,128)}, bf16[2,224,256]{2,1,0:T(8,128)(2,1)}, f32[2,64,224]{2,1,0:T(8,128)}) custom-call(f32[2,224,2048]{2,1,0:T(8,128)} %bitcast.9, bf16[2,128,2048]{2,1,0:T(8,128)(2,1)} %get-tuple-element.13.left_hbm, f32[256,128]{1,0:T(8,128)} %get-tuple-element.14.solve_hbm, ...), custom_call_target="tpu_custom_call" | custom-call | tf_op jit(solution)/shard_map/finish/pallas_call | solution.py:688

commit v6 on v5

--- a/solution.py
+++ b/solution.py
@@ -558,7 +558,7 @@
             jax.ShapeDtypeStruct((256, 128), F32),
             jax.ShapeDtypeStruct((HID, 128), F32),
         ),
-        in_specs=[any_space] * 5,
+        in_specs=[pl.BlockSpec(memory_space=pltpu.HBM)] * 5,
         out_specs=(any_space, any_space, vmem, vmem),
         scratch_shapes=[
             pltpu.VMEM((PAIRS, 4 * CHUNK, DIM), BF16),
@@ -589,14 +589,19 @@
             dma((14,)), dma((14,)), dma((7,)), dma((7,)), pltpu.SemaphoreType.REGULAR((2,)),
         ],
         compiler_params=pltpu.CompilerParams(
-            collective_id=0, has_side_effects=True, vmem_limit_bytes=60 * 1024 * 1024
+            collective_id=0, has_side_effects=True, vmem_limit_bytes=44 * 1024 * 1024
         ),
     )(
-        tokens.reshape(CHUNK, DIM),
-        upstream.reshape(HID, 32 * CHUNK),
-        weight.reshape(2 * HID, DIM),
-        feedback.reshape(2 * HID, DIM),
-        jnp.swapaxes(right_factor, 1, 2),
+        *(
+            pltpu.with_memory_space_constraint(array, pltpu.HBM)
+            for array in (
+                tokens.reshape(CHUNK, DIM),
+                upstream.reshape(HID, 32 * CHUNK),
+                weight.reshape(2 * HID, DIM),
+                feedback.reshape(2 * HID, DIM),
+                jnp.swapaxes(right_factor, 1, 2),
+            )
+        )
     )
 
 
@@ -605,31 +610,16 @@
 
 
 def finish_kernel(
-    delta_hbm, left_hbm, solve_hbm, p_hbm, mom_hbm, w_hbm, fb_out, mom_out, w_out, right_out,
-    delta, left, solve, p, mom, w, wnext, right, coef, in_sem, out_sem,
+    delta, left, solve, p, mom, w, fb_out, mom_out, w_out, right_out,
+    fb, mom_next, w_next, right, coef, out_sem,
 ):
     z = lax.axis_index("rep")
     slab = pl.ds(pl.multiple_of(SLAB * z, SLAB), SLAB)
-    loads = [
-        pltpu.make_async_copy(solve_hbm, solve, in_sem.at[0]),
-        pltpu.make_async_copy(p_hbm, p, in_sem.at[1]),
-    ]
-    loads += [
-        pltpu.make_async_copy(left_hbm.at[t], left.at[pl.ds(2 * RANK * i, 2 * RANK)], in_sem.at[2 + i])
-        for i, t in enumerate((0, 1, 0))
-    ]
-    chunks = [pl.ds(COLS * j, COLS) for j in range(DIM // COLS)]
-    for j, cols in enumerate(chunks):
-        loads.append(
-            pltpu.make_async_copy(delta_hbm.at[:, :, cols], delta.at[:, :, cols], in_sem.at[5 + j])
-        )
-    late = 5 + len(chunks)
-    loads.append(pltpu.make_async_copy(mom_hbm, mom, in_sem.at[late]))
-    loads.append(pltpu.make_async_copy(w_hbm.at[:, :, slab], w, in_sem.at[late + 1]))
-    for copy in loads:
-        copy.start()
-    loads[0].wait()
-    loads[1].wait()
+    stores = []
+
+    def store(src, dst):
+        stores.append(pltpu.make_async_copy(src, dst, out_sem.at[len(stores)]))
+        stores[-1].start()
 
     rows = p[...]
     weights = lax.dot_general(
@@ -642,24 +632,20 @@
         high = own.astype(BF16)
         low = (own - high.astype(F32)).astype(BF16)
         coef[pl.ds(k * HID, HID), :] = jnp.concatenate([high, high, low], axis=1)
-    for copy in loads[2:5]:
-        copy.wait()
 
     def approx_at(cols):
-        return jnp.dot(coef[...], left[:, cols], preferred_element_type=F32)
-
-    stores = []
-
-    def store(src, dst):
-        stores.append(pltpu.make_async_copy(src, dst, out_sem.at[len(stores)]))
-        stores[-1].start()
-
-    for j, cols in enumerate(chunks):
+        return jnp.dot(
+            coef[:, : 4 * RANK], left[:, cols], preferred_element_type=F32
+        ) + jnp.dot(
+            coef[:, 4 * RANK :], left[pl.ds(0, 2 * RANK), cols], preferred_element_type=F32
+        )
+
+    for j in range(DIM // COLS):
+        cols = pl.ds(COLS * j, COLS)
         approx = approx_at(cols)
-        loads[5 + j].wait()
         for k in range(2):
-            delta[k, :, cols] = delta[k, :, cols] - approx[k * HID : (k + 1) * HID]
-        store(delta.at[:, :, cols], fb_out.at[:, :, cols])
+            fb[k, :, cols] = delta[k, :, cols] - approx[k * HID : (k + 1) * HID]
+        store(fb.at[:, :, cols], fb_out.at[:, :, cols])
         if j == 0:
             turned = lax.dot_general(
                 solve[pl.ds(0, 2 * RANK), :], rows, NT,
@@ -669,27 +655,23 @@
             right[1] = turned[RANK:]
             store(right, right_out)
             approx = approx_at(slab)
-            loads[late].wait()
-            loads[late + 1].wait()
             for k in range(2):
                 moved = momentum_decay * mom[k] + approx[k * HID : (k + 1) * HID]
-                mom[k] = moved
-                wnext[k] = (w[k].astype(F32) - step_rate * moved).astype(BF16)
-            store(mom, mom_out)
-            store(wnext, w_out)
+                mom_next[k] = moved
+                w_next[k] = (w[k, :, slab].astype(F32) - step_rate * moved).astype(BF16)
+            store(mom_next, mom_out)
+            store(w_next, w_out)
     for copy in stores:
         copy.wait()
 
 
-def finish_call(delta, left, solve, p, momentum, weight):
-    any_space = pl.BlockSpec(memory_space=pl.ANY)
+def finish_call(*arrays):
     dma = pltpu.SemaphoreType.DMA
-    n = DIM // COLS
     return pl.pallas_call(
         finish_kernel,
         name="finish",
-        in_specs=[any_space] * 6,
-        out_specs=(any_space,) * 4,
+        in_specs=[pl.BlockSpec(memory_space=pltpu.VMEM)] * 6,
+        out_specs=(pl.BlockSpec(memory_space=pl.ANY),) * 4,
         out_shape=(
             jax.ShapeDtypeStruct((2, HID, DIM), F32),
             jax.ShapeDtypeStruct((2, HID, SLAB), F32),
@@ -698,24 +680,20 @@
         ),
         scratch_shapes=[
             pltpu.VMEM((2, HID, DIM), F32),
-            pltpu.VMEM((6 * RANK, DIM), BF16),
-            pltpu.VMEM((256, 128), F32),
-            pltpu.VMEM((HID, 128), F32),
             pltpu.VMEM((2, HID, SLAB), F32),
-            pltpu.VMEM((2, HID, SLAB), BF16),
             pltpu.VMEM((2, HID, SLAB), BF16),
             pltpu.VMEM((2, RANK, HID), F32),
             pltpu.VMEM((2 * HID, 6 * RANK), BF16),
-            dma((n + 7,)), dma((n + 3,)),
+            dma((DIM // COLS + 3,)),
         ],
-        compiler_params=pltpu.CompilerParams(vmem_limit_bytes=60 * 1024 * 1024),
-    )(delta, left, solve, p, momentum, weight)
+        compiler_params=pltpu.CompilerParams(vmem_limit_bytes=24 * 1024 * 1024),
+    )(*(pltpu.with_memory_space_constraint(array, pltpu.VMEM) for array in arrays))
 
 
 def per_device(tokens, upstream, weight, feedback, momentum, right_factor):
     delta, left, solve, p = step_call(tokens, upstream, weight, feedback, right_factor)
     feedback_next, momentum_next, weight_next, right_next = finish_call(
-        delta.reshape(2, HID, DIM), left, solve, p, momentum, weight
+        delta.reshape(2, HID, DIM), left.reshape(4 * RANK, DIM), solve, p, momentum, weight
     )
     return (feedback_next[None], momentum_next, weight_next, jnp.swapaxes(right_next, 1, 2))
 

time: 115 us -> 113 us (0.983)
  Pallas kernels: 115 us -> 112 us
    pallas_call x1, Pallas kernels: 5.5 us -> 3.18 us  [finish_call(): pl.pallas_call(finish_kernel, name='finish', in_specs=[pl.BlockSpec(memor...]
where the time goes in v6:
time: 113 us
  Pallas kernels  112 us (99%)
    pallas_call x1, Pallas kernels, step_call(): pl.pallas_call(step_kernel, name='gather_reduce', out_shape=(jax.ShapeDty...  109 us
    pallas_call x1, Pallas kernels, finish_call(): pl.pallas_call(finish_kernel, name='finish', in_specs=[pl.BlockSpec(memor...  3.18 us

profile of v6, /device:TPU:1, one launch (start us, length us, event | category | flops | bytes accessed | tf_op | source)
XLA Modules:
  0.0 112.6 jit_solution(7122040484041349232)
XLA Ops:
  0.6 0.0 copy-start
  0.6 0.0 copy-start.1
  0.7 108.7 %gather_reduce.1 = (f32[448,2048]{1,0:T(8,128)S(1)}, bf16[2,128,2048]{2,1,0:T(8,128)(2,1)S(1)}, f32[256,128]{1,0:T(8,128)S(1)}, f32[224,128]{1,0:T(8,128)S(1)}) custom-call(bf16[128,2048]{1,0:T(8,128)(2,1)} %bitcast.14, bf16[224,4096]{1,0:T(8,128)(2,1)} %bitcast.13, bf16[448,2048]{1,0:T(8,128)(2,1)} %bitcast.9, f32[448,2048]{1,0:T(8,128)} %bitcast.12, ...), custom_call_target="tpu_custom_call" | custom-call | tf_op jit(solution)/shard_map/gather_reduce/pallas_call | solution.py:552
  109.4 0.0 copy-done
  109.4 0.0 copy-done.1
  109.4 3.2 %finish.1 = (f32[2,224,2048]{2,1,0:T(8,128)}, f32[2,224,256]{2,1,0:T(8,128)}, bf16[2,224,256]{2,1,0:T(8,128)(2,1)}, f32[2,64,224]{2,1,0:T(8,128)}) custom-call(f32[2,224,2048]{2,1,0:T(8,128)S(1)} %bitcast.10, bf16[256,2048]{1,0:T(8,128)(2,1)S(1)} %bitcast.11, f32[256,128]{1,0:T(8,128)S(1)} %get-tuple-element.14.solve, f32[224,128]{1,0:T(8,128)S(1)} %get-tuple-element.15.p, ...), custom_call_target="tpu_custom_call" | custom-call | tf_op jit(solution)/shard_map/finish/pallas_call | solution.py:670
Async XLA Ops:
  0.6 108.8 %copy-start = (bf16[2,224,2048]{2,1,0:T(8,128)(2,1)S(1)}, bf16[2,224,2048]{2,1,0:T(8,128)(2,1)}, u32[]{:S(2)}) copy-start(bf16[2,224,2048]{2,1,0:T(8,128)(2,1)} %w.1) | copy-start | bytes 5505028
  0.6 108.8 %copy-start.1 = (f32[2,224,256]{2,1,0:T(8,128)S(1)}, f32[2,224,256]{2,1,0:T(8,128)}, u32[]{:S(2)}) copy-start(f32[2,224,256]{2,1,0:T(8,128)} %mom.1) | copy-start | bytes 1376260

commit v7 on v6

--- a/solution.py
+++ b/solution.py
@@ -504,20 +504,24 @@
     for j in range(RANK // 2):
         eliminate(j)
 
-    for slot in range(2):
+    def spread_mean(slot):
         total = psum[slot, p_rows(z), :]
         for off in far_last:
             parts[slot][off].wait_recv()
             total = total + recv4[slot, off - 1]
         pfull[slot, p_rows(z), :] = total * (1.0 / REPS)
-    reps = {}
-    for off in far_first:
-        reps[off] = go(remote(
-            pfull.at[:, p_rows(z), :], pfull.at[:, p_rows(z), :],
-            pg_send.at[off - 1], pg_recv.at[off - 1], rep_peer(off),
-        ))
-
-    for j in range(RANK // 2, RANK):
+        piece_p = pfull.at[slot, p_rows(z), :]
+        out = []
+        for off in far_first:
+            n = 7 * slot + off - 1
+            out.append(go(remote(piece_p, piece_p, pg_send.at[n], pg_recv.at[n], rep_peer(off))))
+        return out
+
+    means = spread_mean(0)
+    for j in range(RANK // 2, 3 * RANK // 4):
+        eliminate(j)
+    means += spread_mean(1)
+    for j in range(3 * RANK // 4, RANK):
         eliminate(j)
 
     inverse0 = jnp.where(lane < RANK, pltpu.roll(tables[0], RANK, 1), 0.0)
@@ -529,8 +533,8 @@
         both.T, both, precision=highest, preferred_element_type=F32
     )
 
-    for off in far_last:
-        reps[off].wait_recv()
+    for copy in means:
+        copy.wait_recv()
     own, other = pfull[0, pl.ds(0, HID // 2), :], pfull[1, pl.ds(0, HID // 2), :]
     gate = jnp.where(c == 0, own, other)
     gate = jnp.concatenate([gate, pltpu.roll(gate, RANK, 1)], axis=0)
@@ -586,7 +590,7 @@
             dma((AG_SENDS,)), dma((UNITS, 2)), dma((UNITS,)), dma((UNITS,)),
             dma((4,)), dma((4,)), dma((6,)), dma((6,)), dma((3,)), dma((3,)), dma((7,)), dma((7,)),
             dma((7,)), dma((7,)), dma((3,)), dma((3,)), dma((3,)), dma((3,)), dma((4,)), dma((4,)),
-            dma((14,)), dma((14,)), dma((7,)), dma((7,)), pltpu.SemaphoreType.REGULAR((2,)),
+            dma((14,)), dma((14,)), dma((14,)), dma((14,)), pltpu.SemaphoreType.REGULAR((2,)),
         ],
         compiler_params=pltpu.CompilerParams(
             collective_id=0, has_side_effects=True, vmem_limit_bytes=44 * 1024 * 1024

time: 113 us -> 113 us (level)
  no operation moved by 1% of the time
where the time goes in v7:
time: 113 us
  Pallas kernels  112 us (99%)
    pallas_call x1, Pallas kernels, step_call(): pl.pallas_call(step_kernel, name='gather_reduce', out_shape=(jax.ShapeDty...  109 us
    pallas_call x1, Pallas kernels, finish_call(): pl.pallas_call(finish_kernel, name='finish', in_specs=[pl.BlockSpec(memor...  3.18 us

profile of v7, /device:TPU:1, one launch (start us, length us, event | category | flops | bytes accessed | tf_op | source)
XLA Modules:
  0.0 112.6 jit_solution(11954179146226116393)
XLA Ops:
  0.6 0.0 copy-start
  0.6 0.0 copy-start.1
  0.7 108.7 %gather_reduce.1 = (f32[448,2048]{1,0:T(8,128)S(1)}, bf16[2,128,2048]{2,1,0:T(8,128)(2,1)S(1)}, f32[256,128]{1,0:T(8,128)S(1)}, f32[224,128]{1,0:T(8,128)S(1)}) custom-call(bf16[128,2048]{1,0:T(8,128)(2,1)} %bitcast.14, bf16[224,4096]{1,0:T(8,128)(2,1)} %bitcast.13, bf16[448,2048]{1,0:T(8,128)(2,1)} %bitcast.9, f32[448,2048]{1,0:T(8,128)} %bitcast.12, ...), custom_call_target="tpu_custom_call" | custom-call | tf_op jit(solution)/shard_map/gather_reduce/pallas_call | solution.py:556
  109.4 0.0 copy-done
  109.4 0.0 copy-done.1
  109.4 3.2 %finish.1 = (f32[2,224,2048]{2,1,0:T(8,128)}, f32[2,224,256]{2,1,0:T(8,128)}, bf16[2,224,256]{2,1,0:T(8,128)(2,1)}, f32[2,64,224]{2,1,0:T(8,128)}) custom-call(f32[2,224,2048]{2,1,0:T(8,128)S(1)} %bitcast.10, bf16[256,2048]{1,0:T(8,128)(2,1)S(1)} %bitcast.11, f32[256,128]{1,0:T(8,128)S(1)} %get-tuple-element.14.solve, f32[224,128]{1,0:T(8,128)S(1)} %get-tuple-element.15.p, ...), custom_call_target="tpu_custom_call" | custom-call | tf_op jit(solution)/shard_map/finish/pallas_call | solution.py:674
Async XLA Ops:
  0.6 108.8 %copy-start = (bf16[2,224,2048]{2,1,0:T(8,128)(2,1)S(1)}, bf16[2,224,2048]{2,1,0:T(8,128)(2,1)}, u32[]{:S(2)}) copy-start(bf16[2,224,2048]{2,1,0:T(8,128)(2,1)} %w.1) | copy-start | bytes 5505028
  0.6 108.8 %copy-start.1 = (f32[2,224,256]{2,1,0:T(8,128)S(1)}, f32[2,224,256]{2,1,0:T(8,128)}, u32[]{:S(2)}) copy-start(f32[2,224,256]{2,1,0:T(8,128)} %mom.1) | copy-start | bytes 1376260
